TPU v7x, 32 devices: a whole 2x2x4 slice. The times are simulated.
32 devices in a mesh: parts: 2 (over y), frame: 4 (over z), row: 4 (over x, core).
Axes of the slice: x: 2, y: 2, z: 4, core: 2. Of those that a mesh axis runs over, the one named last changes fastest.
Arguments:
- features: bfloat16 [4, 4, 32, 32, 128], P('parts', 'frame', 'row'), parts along dimension 0, may hold values from -6 to 6
- w_in: bfloat16 [2, 3, 3, 256, 128], replicated, as said below
- b_in: float32 [2, 128], replicated, may hold values from -3 to 3
- w_mid: bfloat16 [2, 3, 3, 128, 128], replicated, may hold values from -0.1875 to 0.1875
- b_mid: float32 [2, 128], replicated, may hold values from -3 to 3
- w_out: bfloat16 [2, 3, 3, 128, 128], replicated, may hold values from -0.1875 to 0.1875
- b_out: float32 [2, 128], replicated, may hold values from -3 to 3
Outputs:
- forward_states: bfloat16 [4, 4, 32, 32, 128], P('parts', 'frame', 'row'), parts along dimension 0
- backward_states: bfloat16 [4, 4, 32, 32, 128], P('parts', 'frame', 'row'), parts along dimension 0
There are 2 independent parts, one for each index of `parts`. A program takes and returns all parts, laid end to end along the dimension named above; an argument that names none is the same for every part. Nothing has to cross between parts.
Inputs may be any that keep to these rules, and one draw needn't show every extreme that they name: `w_in`: weights of the first convolutions.
All inputs are finite; a program needn't handle non-finite values.
Results may differ from a plain program's by a relative error of at most 0.014.
Values may be sent and summed in bfloat16 or wider, within the bound.
No kernel may reach another device: no remote copies, remote signals or barrier semaphores. Data moves between devices by JAX's collectives and lax.ppermute only.
A program may use at most 64 MiB of HBM per device.

v0:
```python
import functools

import jax
import jax.numpy as jnp
from jax import lax
from jax.experimental import pallas as pl
from jax.experimental.pallas import tpu as pltpu
from jax.sharding import PartitionSpec as P


def gelu(v):
    return 0.5 * v * (1.0 + lax.erf(v * 0.7071067811865476))


def widen(rows):
    cols = rows.shape[1]
    col = lax.broadcasted_iota(jnp.int32, rows.shape, 1)
    left = jnp.where(col == 0, 0.0, pltpu.roll(rows, 1, 1))
    right = jnp.where(col == cols - 1, 0.0, pltpu.roll(rows, cols - 1, 1))
    return jnp.concatenate([left, rows, right], axis=-1).astype(jnp.bfloat16)


class Field:
    def __init__(self, even, odd):
        self.even, self.odd = even, odd

    def clear(self):
        self.odd[0] = jnp.zeros(self.odd.shape[1:], self.odd.dtype)

    def zero_row(self, row):
        self.even[row // 2] = jnp.zeros(self.even.shape[1:], self.even.dtype)

    def put_row(self, row, value):
        wide = widen(value.astype(jnp.float32)[None])[0]
        if row % 2 == 0:
            self.even[row // 2] = wide
        else:
            self.odd[row // 2 + 1] = wide

    def put_pairs(self, lo, hi, first, second):
        self.even[lo:hi] = widen(first)
        self.odd[lo + 1 : hi + 1] = widen(second)

    def patches(self, lo, hi):
        n = hi - lo
        cols, wide = self.even.shape[1:]
        parts = [self.odd[lo:hi], self.even[lo:hi], self.odd[lo + 1 : hi + 1], self.even[lo + 1 : hi + 1]]
        return jnp.concatenate(parts, axis=-1).reshape(n * cols, 4 * wide)

    def centre(self, lo, hi):
        ch = self.even.shape[2] // 3
        return (
            self.even[lo:hi, :, ch : 2 * ch].astype(jnp.float32),
            self.odd[lo + 1 : hi + 1, :, ch : 2 * ch].astype(jnp.float32),
        )


def conv_pairs(field, weight, lo, hi):
    out = jnp.dot(field.patches(lo, hi), weight[...], preferred_element_type=jnp.float32)
    return out.reshape(hi - lo, field.even.shape[1], weight.shape[-1])


def split(acc, bias):
    ch = acc.shape[-1] // 2
    return acc[:, :, :ch] + bias, acc[:, :, ch:] + bias


SPLIT = 7


def run(stages):
    waiting = []

    def finish_to(count):
        while len(waiting) > count:
            done = waiting.pop(0)
            done[0](*done[1:])

    for s, (pairs, sums, finish) in enumerate(stages):
        edge = min(max(SPLIT - s, 0), pairs)
        if edge == 0 or edge == pairs:
            finish_to(0)
            waiting.append((finish, 0, pairs, sums(0, pairs)))
            continue
        finish_to(1)
        waiting.append((finish, 0, edge, sums(0, edge)))
        finish_to(1)
        waiting.append((finish, edge, pairs, sums(edge, pairs)))
    finish_to(0)


def frame_stages(first_sums, sizes, first, middle, w_mid, w_out, b_in, b_mid, b_out, emit):
    def activated(field, bias):
        def finish(lo, hi, acc):
            a, b = split(acc, bias)
            field.put_pairs(lo, hi, gelu(a), gelu(b))

        return finish

    def add(lo, hi, acc):
        a, b = split(acc, b_out)
        ra, rb = first.centre(lo, hi)
        emit(lo, hi, (ra + a).astype(jnp.bfloat16), (rb + b).astype(jnp.bfloat16))

    return [
        (sizes[0], first_sums, activated(first, b_in)),
        (sizes[1], lambda lo, hi: conv_pairs(first, w_mid, lo, hi), activated(middle, b_mid)),
        (sizes[2], lambda lo, hi: conv_pairs(middle, w_out, lo, hi), add),
    ]


def pair_sizes(rows):
    return (rows + 3) // 2, (rows + 2) // 2, (rows + 1) // 2


def load_either(field, rows, flip, pick, a, b, height):
    depth = a[1].shape[0]
    for i in range(rows):
        if i < height:
            at, k = jnp.where(flip, height - 1 - i, i), 0
        else:
            at, k = jnp.where(flip, depth - 1 - (i - height), i - height), 1
        field.put_row(i, jnp.where(pick, a[k][at].astype(jnp.float32), b[k][at].astype(jnp.float32)))


def pack_kernel(phase, parts, flags, *refs):
    flip = flags[0] == 1
    direction = flags[2] if phase == 0 else 1 - flags[2]
    packed = refs[-1]
    ch = packed.shape[-1] // 2
    zero = jnp.zeros((3 * ch, ch), packed.dtype)
    for conv, (which, base) in enumerate(parts):
        packed[conv, 9 * ch : 12 * ch, :ch] = zero
        packed[conv, : 3 * ch, ch:] = zero
        for dy in range(3):
            at = jnp.where(flip, 2 - dy, dy)
            for dx in range(3):
                taps = refs[which][direction, at, dx, base : base + ch, :]
                for o in range(2):
                    row = 3 * ch * (dy + o) + ch * dx
                    packed[conv, row : row + ch, o * ch : (o + 1) * ch] = taps


def pack_weights(phase, parts, flags, *weights):
    ch = weights[0].shape[-1]
    return pl.pallas_call(
        functools.partial(pack_kernel, phase, parts),
        out_shape=jax.ShapeDtypeStruct((len(parts), 12 * ch, 2 * ch), weights[0].dtype),
        in_specs=[SMEM] + [VMEM] * len(weights),
        out_specs=VMEM,
        cost_estimate=pl.CostEstimate(flops=0, bytes_accessed=8 << 20, transcendentals=0),
        compiler_params=pltpu.CompilerParams(vmem_limit_bytes=12 << 20),
    )(flags, *weights)


def pack_phase(phase, flags, w_in, w_mid, w_out):
    ch = w_mid.shape[-1]
    outer = pack_weights(phase, ((0, 0), (0, ch)), flags, w_in)
    flags, _ = lax.optimization_barrier((flags, outer))
    return outer, pack_weights(phase, ((0, 0), (1, 0)), flags, w_mid, w_out)


def fields_of(refs):
    return [Field(refs[2 * i], refs[2 * i + 1]) for i in range(len(refs) // 2)]


def biases_of(direction, *refs):
    return [jnp.where(direction == 1, ref[1], ref[0]) for ref in refs]


def store_canonical(ref, flip, height, lo, hi, a, b, keep=None):
    for p in range(lo, hi):
        for o, v in ((0, a), (1, b)):
            i = 2 * p + o
            if i < height:
                at = jnp.where(flip, height - 1 - i, i)
                ref[at] = v[p - lo] if keep is None else jnp.where(keep, ref[at].astype(jnp.float32), v[p - lo].astype(jnp.float32)).astype(ref.dtype)


def first_kernel(height, flags, near_own, far_own, near_other, far_other, outer, inner, b_in, b_mid, b_out, state, result, *scratch):
    flip, own_first = flags[0] == 1, flags[1] == 1
    bias = biases_of(flags[2], b_in, b_mid, b_out)
    w_f, w_s, w_m, w_o = outer.at[0], outer.at[1], inner.at[0], inner.at[1]
    frame0, frame1, held, first0, middle0, first1, middle1 = fields = fields_of(scratch)
    for f in fields:
        f.clear()
    own, other = (near_own, far_own), (near_other, far_other)
    load_either(frame0, height + 6, flip, own_first, own, other, height)
    load_either(frame1, height + 3, flip, own_first, other, own, height)

    def emit_first(lo, hi, a, b):
        held.put_pairs(lo, hi, a.astype(jnp.float32), b.astype(jnp.float32))
        store_canonical(result, flip, height, lo, hi, a, b)

    def emit_second(lo, hi, a, b):
        for p in range(lo, hi):
            state[2 * p] = a[p - lo]
            state[2 * p + 1] = b[p - lo]
        store_canonical(result, flip, height, lo, hi, a, b, keep=own_first)

    def second_sums(lo, hi):
        return conv_pairs(frame1, w_f, lo, hi) + conv_pairs(held, w_s, lo, hi)

    n0, n1 = pair_sizes(height + 3), pair_sizes(height)
    frame0.zero_row(2 * n0[0])
    middle0.zero_row(2 * n0[2])
    first1.zero_row(2 * n1[0])
    run(
        frame_stages(lambda lo, hi: conv_pairs(frame0, w_f, lo, hi), n0, first0, middle0, w_m, w_o, *bias, emit_first)
        + frame_stages(second_sums, n1, first1, middle1, w_m, w_o, *bias, emit_second)
    )


def ahead_kernel(height, flags, near_own, far_own, near_other, far_other, outer, sums0, sums1, *scratch):
    flip, own_first = flags[0] == 1, flags[1] == 1
    frame0, frame1 = fields_of(scratch)
    for f in (frame0, frame1):
        f.clear()
    own, other = (near_own, far_own), (near_other, far_other)
    load_either(frame0, height + 6, flip, own_first, other, own, height)
    frame0.zero_row(2 * sums0.shape[0])
    load_either(frame1, height + 3, flip, own_first, own, other, height)
    for field, sums in ((frame0, sums0), (frame1, sums1)):
        sums[...] = conv_pairs(field, outer.at[0], 0, sums.shape[0])


def second_kernel(height, flags, near, far, sums0, sums1, outer, inner, b_in, b_mid, b_out, result, *scratch):
    flip, own_first = flags[0] == 1, flags[1] == 1
    bias = biases_of(1 - flags[2], b_in, b_mid, b_out)
    w_s, w_m, w_o = outer.at[1], inner.at[0], inner.at[1]
    state, held, first0, middle0, first1, middle1 = fields = fields_of(scratch)
    for f in fields:
        f.clear()
    depth = far.shape[0]
    for i in range(height):
        state.put_row(i, near[i])
    for i in range(depth):
        state.put_row(height + i, far[depth - 1 - i])
    state.zero_row(height + depth)

    def emit_first(lo, hi, a, b):
        held.put_pairs(lo, hi, a.astype(jnp.float32), b.astype(jnp.float32))
        store_canonical(result, flip, height, lo, hi, a, b)

    def emit_second(lo, hi, a, b):
        store_canonical(result, flip, height, lo, hi, a, b, keep=jnp.logical_not(own_first))

    n0, n1 = pair_sizes(height + 3), pair_sizes(height)
    middle0.zero_row(2 * n0[2])
    first1.zero_row(2 * n1[0])
    run(
        frame_stages(lambda lo, hi: sums0[lo:hi] + conv_pairs(state, w_s, lo, hi), n0, first0, middle0, w_m, w_o, *bias, emit_first)
        + frame_stages(lambda lo, hi: sums1[lo:hi] + conv_pairs(held, w_s, lo, hi), n1, first1, middle1, w_m, w_o, *bias, emit_second)
    )


VMEM = pl.BlockSpec(memory_space=pltpu.VMEM)
SMEM = pl.BlockSpec(memory_space=pltpu.SMEM)
LIMIT = 24 << 20


def field_scratch(count, rows, cols, ch):
    return [pltpu.VMEM((rows // 2 + 1, cols, 3 * ch), jnp.bfloat16) for _ in range(2 * count)]


def paired(features, w_in, b_in, w_mid, b_mid, w_out, b_out):
    _, _, slab, cols, ch = features.shape
    height = 2 * slab
    depth = 6
    where_row, owner = lax.axis_index("row"), lax.axis_index("frame")
    core, column = where_row % 2, where_row // 2
    own_first = ((owner == 0) | (owner == 3)).astype(jnp.int32)
    late = (owner >= 2).astype(jnp.int32)
    flags = jnp.stack([column, own_first, late])
    swap_core = [(0, 1), (1, 0), (2, 3), (3, 2)]
    swap_column = [(0, 2), (2, 0), (1, 3), (3, 1)]
    swap_near = [(0, 1), (1, 0), (2, 3), (3, 2)]
    cross = [(0, 2), (2, 0), (1, 3), (3, 1)]
    cross_both = [(4 * f + r, 4 * (f ^ 2) + (r ^ 2)) for f in range(4) for r in range(4)]
    swap_both = [(4 * f + r, 4 * (f ^ 1) + (r ^ 2)) for f in range(4) for r in range(4)]

    biases = (b_in, b_mid, b_out)
    mine = features[:, 0]
    kept = lax.dynamic_index_in_dim(mine, core, 0, keepdims=False)
    got = lax.ppermute(lax.dynamic_index_in_dim(mine, 1 - core, 0, keepdims=False), "row", swap_core)
    near_own = jnp.where(core == 0, jnp.concatenate([kept, got]), jnp.concatenate([got, kept]))
    edge = lax.dynamic_slice_in_dim(near_own, (height - depth) * (1 - column), depth, 0)
    near_other = lax.ppermute(near_own, "frame", swap_near)
    far_own = lax.ppermute(edge, "row", swap_column)
    far_other = lax.ppermute(edge, ("frame", "row"), swap_both)
    frames = (near_own, far_own, near_other, far_other)

    rows = height + 8
    bf16 = jnp.bfloat16
    cost = lambda rows: pl.CostEstimate(flops=rows * cols * ch * ch * 24, bytes_accessed=4 << 20, transcendentals=0)
    held_flags, _ = lax.optimization_barrier((flags, near_own))
    packed = pack_phase(0, held_flags, w_in, w_mid, w_out)
    state, early = pl.pallas_call(
        functools.partial(first_kernel, height),
        grid=(1,),
        out_shape=(
            jax.ShapeDtypeStruct((height, cols, ch), bf16),
            jax.ShapeDtypeStruct((height, cols, ch), bf16),
        ),
        in_specs=[SMEM] + [VMEM] * 9,
        out_specs=(VMEM, VMEM),
        scratch_shapes=field_scratch(7, rows, cols, ch),
        cost_estimate=cost(190),
        compiler_params=pltpu.CompilerParams(vmem_limit_bytes=LIMIT),
    )(flags, *frames, *packed, *biases)

    incoming = lax.ppermute(state, "frame", cross)
    edge = lax.ppermute(state[height - depth :], ("frame", "row"), cross_both)
    held_flags, _ = lax.optimization_barrier((flags, state))
    packed = pack_phase(1, held_flags, w_in, w_mid, w_out)
    sums = pl.pallas_call(
        functools.partial(ahead_kernel, height),
        grid=(1,),
        out_shape=tuple(jax.ShapeDtypeStruct((n, cols, 2 * ch), jnp.float32) for n in ((height + 6) // 2, (height + 3) // 2)),
        in_specs=[SMEM] + [VMEM] * 5,
        out_specs=(VMEM, VMEM),
        scratch_shapes=field_scratch(2, rows, cols, ch),
        cost_estimate=cost(42),
        compiler_params=pltpu.CompilerParams(vmem_limit_bytes=LIMIT),
    )(flags, *frames, packed[0])
    later = pl.pallas_call(
        functools.partial(second_kernel, height),
        grid=(1,),
        out_shape=jax.ShapeDtypeStruct((height, cols, ch), bf16),
        in_specs=[SMEM] + [VMEM] * 9,
        out_specs=VMEM,
        scratch_shapes=field_scratch(6, rows, cols, ch),
        cost_estimate=cost(120),
        compiler_params=pltpu.CompilerParams(vmem_limit_bytes=LIMIT),
    )(flags, incoming, edge, *sums, *packed, *biases)

    both = jnp.stack([early, later])
    kept = lax.dynamic_slice_in_dim(both, slab * core, slab, 1)
    got = lax.ppermute(lax.dynamic_slice_in_dim(both, slab * (1 - core), slab, 1), "row", swap_core)
    by_clip = jnp.where(core == 0, jnp.stack([kept, got], 1), jnp.stack([got, kept], 1))
    forward = jnp.where(late == 1, by_clip[1], by_clip[0])
    backward = jnp.where(late == 1, by_clip[0], by_clip[1])
    return forward[:, None], backward[:, None]


def with_halo(block, sides, width):
    for axis, dim in sides:
        count = lax.axis_size(axis)
        forward = [(i, i + 1) for i in range(count - 1)]
        backward = [(target, source) for source, target in forward]
        low = lax.ppermute(
            lax.slice_in_dim(block, block.shape[dim] - width, None, axis=dim), axis, forward
        )
        high = lax.ppermute(lax.slice_in_dim(block, 0, width, axis=dim), axis, backward)
        block = jnp.concatenate([low, block, high], axis=dim)
    return block


def shifted(shard, axis, by):
    length = lax.axis_size(axis)
    pairs = [(i, i + by) for i in range(length) if 0 <= i + by < length]
    return lax.ppermute(shard, axis, pairs)


def conv_layer(field, weight, bias_vec):
    padded = jnp.pad(field, ((0, 0), (1, 1), (0, 0)))
    row_count = padded.shape[0] - 2
    col_count = padded.shape[1] - 2
    summed = jnp.zeros((row_count, col_count, weight.shape[-1]), jnp.float32)
    for offset_y in range(3):
        for offset_x in range(3):
            window = padded[offset_y : offset_y + row_count, offset_x : offset_x + col_count, :]
            product = jnp.dot(
                window.reshape(row_count * col_count, window.shape[-1]),
                weight[offset_y, offset_x],
                preferred_element_type=jnp.float32,
            )
            summed = summed + product.reshape(row_count, col_count, weight.shape[-1])
    return summed + bias_vec


def activate(values):
    return jax.nn.gelu(values, approximate=False)


def pipelined(features, w_in, b_in, w_mid, b_mid, w_out, b_out):
    clip_count, frame_count, row_count, col_count, channels = features.shape
    owners = lax.axis_size("frame")
    owner_pos = lax.axis_index("frame")
    section_total = owners + clip_count - 1
    rim_depth = 3
    rimmed = with_halo(features, (("row", 2),), rim_depth)
    slab_start = lax.axis_index("row") * row_count
    total_rows = row_count * lax.axis_size("row")
    outer_rows = slab_start - 2 + jnp.arange(row_count + 4, dtype=jnp.int32)
    outer_mask = ((outer_rows >= 0) & (outer_rows < total_rows)).astype(jnp.float32)[:, None, None]
    inner_rows = slab_start - 1 + jnp.arange(row_count + 2, dtype=jnp.int32)
    inner_mask = ((inner_rows >= 0) & (inner_rows < total_rows)).astype(jnp.float32)[:, None, None]
    zero_state = jnp.zeros((row_count, col_count, channels), jnp.bfloat16)

    def skipped(operand):
        return zero_state

    def frame_step(frame_rim, carried, direction, is_live):
        state_rim = with_halo(carried, (("row", 0),), rim_depth)
        joined = jnp.concatenate([frame_rim, state_rim], axis=-1)

        def compute(joined_in):
            first_act = (
                activate(conv_layer(joined_in, w_in[direction], b_in[direction])) * outer_mask
            ).astype(jnp.bfloat16)
            middle = (
                activate(conv_layer(first_act, w_mid[direction], b_mid[direction])) * inner_mask
            ).astype(jnp.bfloat16)
            residual = first_act[2:-2].astype(jnp.float32)
            return (residual + conv_layer(middle, w_out[direction], b_out[direction])).astype(
                jnp.bfloat16
            )

        return lax.cond(is_live, compute, skipped, joined)

    def sweep_section(section_num, incoming, outputs, direction):
        position = owner_pos if direction == 0 else owners - 1 - owner_pos
        clip_index = section_num - position
        is_live = (clip_index >= 0) & (clip_index < clip_count)
        chosen = jnp.clip(clip_index, 0, clip_count - 1)
        clip_frames = lax.dynamic_index_in_dim(rimmed, chosen, 0, keepdims=False)
        clip_out = lax.dynamic_index_in_dim(outputs, chosen, 0, keepdims=False)
        carried = incoming
        frame_order = range(frame_count) if direction == 0 else range(frame_count - 1, -1, -1)
        for frame_slot in frame_order:
            carried = frame_step(clip_frames[frame_slot], carried, direction, is_live)
            clip_out = clip_out.at[frame_slot].set(
                jnp.where(is_live, carried, clip_out[frame_slot])
            )
        outputs = lax.dynamic_update_index_in_dim(outputs, clip_out, chosen, 0)
        if direction == 0:
            passed = shifted(carried, "frame", 1)
        else:
            passed = shifted(carried, "frame", -1)
        return (passed, outputs)

    blank_out = jnp.zeros_like(features)

    def forward_turn(section_num, carry):
        return sweep_section(section_num, carry[0], carry[1], 0)

    def backward_turn(section_num, carry):
        return sweep_section(section_num, carry[0], carry[1], 1)

    _, forward_states = lax.fori_loop(0, section_total, forward_turn, (zero_state, blank_out))
    _, backward_states = lax.fori_loop(0, section_total, backward_turn, (zero_state, blank_out))
    return (forward_states, backward_states)


def on_device(features, *weights):
    clips, frames, slab, _, _ = features.shape
    fits = (clips, frames, lax.axis_size("frame"), lax.axis_size("row")) == (2, 1, 4, 4) and slab >= 6
    return (paired if fits else pipelined)(features, *weights)


def solution(mesh):
    placed = (P("parts", "frame", "row", None, None), P(), P(), P(), P(), P(), P())

    return jax.shard_map(
        on_device,
        mesh=mesh,
        in_specs=placed,
        out_specs=(P("parts", "frame", "row", None, None), P("parts", "frame", "row", None, None)),
        check_vma=False,
    )
```

profile of v0, /device:TPU:0, one launch (start us, length us, event | category | flops | bytes accessed | tf_op | source)
XLA Modules:
  0.0 31.5 jit_solution(7623477756108412649)
XLA Ops:
  0.7 0.9 %dynamic-slice_bitcast_fusion.1 = (bf16[8,32,128]{2,1,0:T(8,128)(2,1)S(1)}, bf16[8,32,128]{2,1,0:T(8,128)(2,1)S(1)}) fusion(bf16[2,1,8,32,128]{4,3,2,1,0:T(8,128)(2,1)} %param.7, s32[]{:T(128)S(6)} %select_n.80, s32[]{:T(128)S(6)} %select_n.81), kind=kLoop, calls=%fused_computation.12 | loop fusion | bytes 262152 | tf_op jit(solution)/shard_map/jit(dynamic_index_in_dim)/squeeze | solution.py:284
  1.6 0.6 %collective-permute-start = (bf16[8,32,128]{2,1,0:T(8,128)(2,1)S(1)}, bf16[8,32,128]{2,1,0:T(8,128)(2,1)S(1)}, u32[]{:S(2)}, u32[]{:S(2)}) collective-permute-start(bf16[8,32,128]{2,1,0:T(8,128)(2,1)S(1)} %get-tuple-element.25), channel_id=1, source_target_pairs={{0,1},{1,0},{2,3},{3,2},{4,5},{5,4},{6,7},{7,6},{8,9},{9,8},{10,11... | collective-permute-start | bytes 196616 | tf_op jit(solution)/shard_map/ppermute | solution.py:285
  2.2 0.9 %collective-permute-done = bf16[8,32,128]{2,1,0:T(8,128)(2,1)S(1)} collective-permute-done((bf16[8,32,128]{2,1,0:T(8,128)(2,1)S(1)}, bf16[8,32,128]{2,1,0:T(8,128)(2,1)S(1)}, u32[]{:S(2)}, u32[]{:S(2)}) %collective-permute-start) | collective-permute-done | bytes 65568 | tf_op jit(solution)/shard_map/ppermute | solution.py:285
  3.1 3.0 %collective-permute-start.2 = (bf16[16,32,128]{2,1,0:T(8,128)(2,1)S(1)}, bf16[16,32,128]{2,1,0:T(8,128)(2,1)S(1)}, u32[]{:S(2)}, u32[]{:S(2)}) collective-permute-start(bf16[16,32,128]{2,1,0:T(8,128)(2,1)S(1)} %maximum_select_fusion.1.near_own), channel_id=1, source_target_pairs={{0,4},{4,0},{8,12},{12,8},{1,5},{5,1},{9,13},{13,9},{2,6},{6,2},{1... | collective-permute-start | bytes 393224 | tf_op jit(solution)/shard_map/ppermute | solution.py:288
  6.1 1.4 %collective-permute-start.3 = (bf16[6,32,128]{2,1,0:T(8,128)(2,1)S(1)}, bf16[6,32,128]{2,1,0:T(8,128)(2,1)S(1)}, u32[]{:S(2)}, u32[]{:S(2)}) collective-permute-start(bf16[6,32,128]{2,1,0:T(8,128)(2,1)S(1)} %constant_dynamic-slice_fusion), channel_id=1, source_target_pairs={{0,6},{1,7},{2,4},{3,5},{4,2},{5,3},{6,0},{7,1},{8,14},{9,15},{10,... | collective-permute-start | bytes 147464 | tf_op jit(solution)/shard_map/ppermute | solution.py:290
  7.5 0.2 collective-permute-start.1
  7.6 0.1 pad_add_fusion.flags
  7.7 1.3 %copy-done = bf16[2,3,3,256,128]{4,3,2,1,0:T(8,128)(2,1)S(1)} copy-done((bf16[2,3,3,256,128]{4,3,2,1,0:T(8,128)(2,1)S(1)}, bf16[2,3,3,256,128]{4,3,2,1,0:T(8,128)(2,1)}, u32[]{:S(2)}) %copy-start) | copy-done | bytes 1179672
  9.0 0.7 %shard_map.86.outer = bf16[2,1536,256]{2,1,0:T(8,128)(2,1)S(1)} custom-call(s32[3]{0:T(128)S(1)} %pad_add_fusion.flags, bf16[2,3,3,256,128]{4,3,2,1,0:T(8,128)(2,1)S(1)} %copy-done), custom_call_target="tpu_custom_call" | custom-call | bytes 8388608 | tf_op jit(solution)/shard_map/pallas_call | solution.py:146
  9.7 0.3 copy-done.3
  10.1 0.7 %shard_map.87.inner = bf16[2,1536,256]{2,1,0:T(8,128)(2,1)S(1)} custom-call(s32[3]{0:T(128)S(1)} %pad_add_fusion.flags, bf16[2,3,3,128,128]{4,3,2,1,0:T(8,128)(2,1)S(1)} %copy-done.2, bf16[2,3,3,128,128]{4,3,2,1,0:T(8,128)(2,1)S(1)} %copy-done.3), custom_call_target="tpu_custom_call" | custom-call | bytes 8388608 | tf_op jit(solution)/shard_map/pallas_call | solution.py:146
  10.8 1.3 %collective-permute-done.3.far_other = bf16[6,32,128]{2,1,0:T(8,128)(2,1)S(1)} collective-permute-done((bf16[6,32,128]{2,1,0:T(8,128)(2,1)S(1)}, bf16[6,32,128]{2,1,0:T(8,128)(2,1)S(1)}, u32[]{:S(2)}, u32[]{:S(2)}) %collective-permute-start.3) | collective-permute-done | bytes 49184 | tf_op jit(solution)/shard_map/ppermute | solution.py:290
  12.1 0.0 collective-permute-done.1.far_own
  12.2 3.4 %shard_map.88 = (bf16[16,32,128]{2,1,0:T(8,128)(2,1)S(1)}, bf16[16,32,128]{2,1,0:T(8,128)(2,1)S(1)}) custom-call(s32[3]{0:T(128)S(1)} %pad_add_fusion.flags, bf16[16,32,128]{2,1,0:T(8,128)(2,1)S(1)} %maximum_select_fusion.1.near_own, bf16[6,32,128]{2,1,0:T(8,128)(2,1)S(1)} %collective-permute-done.1.far_own, ...), custom_call_target="tpu_custom_call" | custom-call | flops 2390753280 | bytes 4194304 | tf_op jit(solution)/shard_map/pallas_call | solution.py:298
  15.6 2.7 %collective-permute-start.4 = (bf16[16,32,128]{2,1,0:T(8,128)(2,1)S(1)}, bf16[16,32,128]{2,1,0:T(8,128)(2,1)S(1)}, u32[]{:S(2)}, u32[]{:S(2)}) collective-permute-start(bf16[16,32,128]{2,1,0:T(8,128)(2,1)S(1)} %get-tuple-element.13), channel_id=1, source_target_pairs={{0,8},{8,0},{4,12},{12,4},{1,9},{9,1},{5,13},{13,5},{2,10},{10,2},... | collective-permute-start | bytes 393224 | tf_op jit(solution)/shard_map/ppermute | solution.py:312
  18.3 0.3 collective-permute-start.5
  18.6 0.7 %shard_map.89.outer = bf16[2,1536,256]{2,1,0:T(8,128)(2,1)S(1)} custom-call(s32[3]{0:T(128)S(1)} %pad_add_fusion.flags, bf16[2,3,3,256,128]{4,3,2,1,0:T(8,128)(2,1)S(1)} %copy-done.1), custom_call_target="tpu_custom_call" | custom-call | bytes 8388608 | tf_op jit(solution)/shard_map/pallas_call | solution.py:146
  19.3 0.7 %shard_map.91.inner = bf16[2,1536,256]{2,1,0:T(8,128)(2,1)S(1)} custom-call(s32[3]{0:T(128)S(1)} %pad_add_fusion.flags, bf16[2,3,3,128,128]{4,3,2,1,0:T(8,128)(2,1)S(1)} %copy-done.2, bf16[2,3,3,128,128]{4,3,2,1,0:T(8,128)(2,1)S(1)} %copy-done.3), custom_call_target="tpu_custom_call" | custom-call | bytes 8388608 | tf_op jit(solution)/shard_map/pallas_call | solution.py:146
  20.1 1.3 %shard_map.90 = (f32[11,32,256]{2,1,0:T(8,128)S(1)}, f32[9,32,256]{2,1,0:T(8,128)S(1)}) custom-call(s32[3]{0:T(128)S(1)} %pad_add_fusion.flags, bf16[16,32,128]{2,1,0:T(8,128)(2,1)S(1)} %maximum_select_fusion.1.near_own, bf16[6,32,128]{2,1,0:T(8,128)(2,1)S(1)} %collective-permute-done.1.far_own, bf16[16,32,128]{2,1,0:T(8,128)(2,1)S(1)} %collective-permute-done.2.near_other, ...), custom_call_target="tpu_custom_call" | custom-call | flops 528482304 | bytes 4194304 | tf_op jit(solution)/shard_map/pallas_call | solution.py:316
  21.4 4.8 %collective-permute-done.5.far = bf16[6,32,128]{2,1,0:T(8,128)(2,1)S(1)} collective-permute-done((bf16[6,32,128]{2,1,0:T(8,128)(2,1)S(1)}, bf16[6,32,128]{2,1,0:T(8,128)(2,1)S(1)}, u32[]{:S(2)}, u32[]{:S(2)}) %collective-permute-start.5) | collective-permute-done | bytes 49184 | tf_op jit(solution)/shard_map/ppermute | solution.py:313
  26.2 3.1 %shard_map.92 = bf16[16,32,128]{2,1,0:T(8,128)(2,1)S(1)} custom-call(s32[3]{0:T(128)S(1)} %pad_add_fusion.flags, bf16[16,32,128]{2,1,0:T(8,128)(2,1)S(1)} %collective-permute-done.4.near, bf16[6,32,128]{2,1,0:T(8,128)(2,1)S(1)} %collective-permute-done.5.far, f32[11,32,256]{2,1,0:T(8,128)S(1)} %get-tuple-element.15.sums0, ...), custom_call_target="tpu_custom_call" | custom-call | flops 1509949440 | bytes 4194304 | tf_op jit(solution)/shard_map/pallas_call | solution.py:326
  29.4 0.1 collective-permute-start.6
  29.4 1.3 %collective-permute-done.6 = bf16[2,8,32,128]{3,2,1,0:T(8,128)(2,1)S(1)} collective-permute-done((bf16[2,8,32,128]{3,2,1,0:T(8,128)(2,1)S(1)}, bf16[2,8,32,128]{3,2,1,0:T(8,128)(2,1)S(1)}, u32[]{:S(2)}, u32[]{:S(2)}) %collective-permute-start.6) | collective-permute-done | bytes 131104 | tf_op jit(solution)/shard_map/ppermute | solution.py:339
  30.8 0.7 %select_bitcast_fusion = (bf16[2,1,8,32,128]{4,3,2,1,0:T(8,128)(2,1)}, bf16[2,1,8,32,128]{4,3,2,1,0:T(8,128)(2,1)}) fusion(pred[]{:T(512)S(6)} %eq.16, bf16[2,2,8,32,128]{4,3,2,0,1:T(8,128)(2,1)S(1)} %maximum_select_fusion), kind=kLoop, calls=%fused_computation.9 | loop fusion | flops 131072 | bytes 524289
  (19 shorter events, 0.1 us)
Async XLA Ops:
  0.7 9.1 %copy-start.2 = (bf16[2,3,3,128,128]{4,3,2,1,0:T(8,128)(2,1)S(1)}, bf16[2,3,3,128,128]{4,3,2,1,0:T(8,128)(2,1)}, u32[]{:S(2)}) copy-start(bf16[2,3,3,128,128]{4,3,2,1,0:T(8,128)(2,1)} %refs_0_.7) | copy-start | bytes 1769476
  1.6 1.5 %collective-permute-start = (bf16[8,32,128]{2,1,0:T(8,128)(2,1)S(1)}, bf16[8,32,128]{2,1,0:T(8,128)(2,1)S(1)}, u32[]{:S(2)}, u32[]{:S(2)}) collective-permute-start(bf16[8,32,128]{2,1,0:T(8,128)(2,1)S(1)} %get-tuple-element.25), channel_id=1, source_target_pairs={{0,1},{1,0},{2,3},{3,2},{4,5},{5,4},{6,7},{7,6},{8,9},{9,8},{10,11... | collective-permute-start | bytes 196616 | tf_op jit(solution)/shard_map/ppermute | solution.py:285
  3.1 9.1 %collective-permute-start.2 = (bf16[16,32,128]{2,1,0:T(8,128)(2,1)S(1)}, bf16[16,32,128]{2,1,0:T(8,128)(2,1)S(1)}, u32[]{:S(2)}, u32[]{:S(2)}) collective-permute-start(bf16[16,32,128]{2,1,0:T(8,128)(2,1)S(1)} %maximum_select_fusion.1.near_own), channel_id=1, source_target_pairs={{0,4},{4,0},{8,12},{12,8},{1,5},{5,1},{9,13},{13,9},{2,6},{6,2},{1... | collective-permute-start | bytes 393224 | tf_op jit(solution)/shard_map/ppermute | solution.py:288
  6.1 6.1 %collective-permute-start.3 = (bf16[6,32,128]{2,1,0:T(8,128)(2,1)S(1)}, bf16[6,32,128]{2,1,0:T(8,128)(2,1)S(1)}, u32[]{:S(2)}, u32[]{:S(2)}) collective-permute-start(bf16[6,32,128]{2,1,0:T(8,128)(2,1)S(1)} %constant_dynamic-slice_fusion), channel_id=1, source_target_pairs={{0,6},{1,7},{2,4},{3,5},{4,2},{5,3},{6,0},{7,1},{8,14},{9,15},{10,... | collective-permute-start | bytes 147464 | tf_op jit(solution)/shard_map/ppermute | solution.py:290
  7.5 4.7 %collective-permute-start.1 = (bf16[6,32,128]{2,1,0:T(8,128)(2,1)S(1)}, bf16[6,32,128]{2,1,0:T(8,128)(2,1)S(1)}, u32[]{:S(2)}, u32[]{:S(2)}) collective-permute-start(bf16[6,32,128]{2,1,0:T(8,128)(2,1)S(1)} %constant_dynamic-slice_fusion), channel_id=1, source_target_pairs={{0,2},{2,0},{1,3},{3,1},{4,6},{6,4},{5,7},{7,5},{8,10},{10,8},{9,1... | collective-permute-start | bytes 147464 | tf_op jit(solution)/shard_map/ppermute | solution.py:289
  7.7 1.3 %copy-start = (bf16[2,3,3,256,128]{4,3,2,1,0:T(8,128)(2,1)S(1)}, bf16[2,3,3,256,128]{4,3,2,1,0:T(8,128)(2,1)}, u32[]{:S(2)}) copy-start(bf16[2,3,3,256,128]{4,3,2,1,0:T(8,128)(2,1)} %refs_0_.6) | copy-start | bytes 3538948
  9.0 1.1 %copy-start.3 = (bf16[2,3,3,128,128]{4,3,2,1,0:T(8,128)(2,1)S(1)}, bf16[2,3,3,128,128]{4,3,2,1,0:T(8,128)(2,1)}, u32[]{:S(2)}) copy-start(bf16[2,3,3,128,128]{4,3,2,1,0:T(8,128)(2,1)} %refs_1_.3) | copy-start | bytes 1769476
  10.0 2.1 %copy-start.4 = (f32[2,128]{1,0:T(2,128)S(1)}, f32[2,128]{1,0:T(2,128)}, u32[]{:S(2)}) copy-start(f32[2,128]{1,0:T(2,128)} %b_in.3) | copy-start | bytes 3076
  10.0 2.1 %copy-start.5 = (f32[2,128]{1,0:T(2,128)S(1)}, f32[2,128]{1,0:T(2,128)}, u32[]{:S(2)}) copy-start(f32[2,128]{1,0:T(2,128)} %b_mid.3) | copy-start | bytes 3076
  10.1 2.1 %copy-start.6 = (f32[2,128]{1,0:T(2,128)S(1)}, f32[2,128]{1,0:T(2,128)}, u32[]{:S(2)}) copy-start(f32[2,128]{1,0:T(2,128)} %b_out.3) | copy-start | bytes 3076
  10.8 7.8 %copy-start.1 = (bf16[2,3,3,256,128]{4,3,2,1,0:T(8,128)(2,1)S(1)}, bf16[2,3,3,256,128]{4,3,2,1,0:T(8,128)(2,1)}, u32[]{:S(2)}) copy-start(bf16[2,3,3,256,128]{4,3,2,1,0:T(8,128)(2,1)} %refs_0_.6) | copy-start | bytes 3538948
  15.6 10.6 %collective-permute-start.4 = (bf16[16,32,128]{2,1,0:T(8,128)(2,1)S(1)}, bf16[16,32,128]{2,1,0:T(8,128)(2,1)S(1)}, u32[]{:S(2)}, u32[]{:S(2)}) collective-permute-start(bf16[16,32,128]{2,1,0:T(8,128)(2,1)S(1)} %get-tuple-element.13), channel_id=1, source_target_pairs={{0,8},{8,0},{4,12},{12,4},{1,9},{9,1},{5,13},{13,5},{2,10},{10,2},... | collective-permute-start | bytes 393224 | tf_op jit(solution)/shard_map/ppermute | solution.py:312
  18.3 7.9 %collective-permute-start.5 = (bf16[6,32,128]{2,1,0:T(8,128)(2,1)S(1)}, bf16[6,32,128]{2,1,0:T(8,128)(2,1)S(1)}, u32[]{:S(2)}, u32[]{:S(2)}) collective-permute-start(bf16[6,32,128]{2,1,0:T(8,128)(2,1)S(1)} %slice.11), channel_id=1, source_target_pairs={{0,10},{1,11},{2,8},{3,9},{4,14},{5,15},{6,12},{7,13},{8,2},{9,3},... | collective-permute-start | bytes 147464 | tf_op jit(solution)/shard_map/ppermute | solution.py:313
  29.4 1.4 %collective-permute-start.6 = (bf16[2,8,32,128]{3,2,1,0:T(8,128)(2,1)S(1)}, bf16[2,8,32,128]{3,2,1,0:T(8,128)(2,1)S(1)}, u32[]{:S(2)}, u32[]{:S(2)}) collective-permute-start(bf16[2,8,32,128]{3,2,1,0:T(8,128)(2,1)S(1)} %get-tuple-element.23), channel_id=1, source_target_pairs={{0,1},{1,0},{2,3},{3,2},{4,5},{5,4},{6,7},{7,6},{8,9},{9,8},{10,11... | collective-permute-start | bytes 393224 | tf_op jit(solution)/shard_map/ppermute | solution.py:339
where the time goes:
time: 31.7 us; the launch traced here: 31.5 us
  Pallas kernels  10.8 us (34%)
  waiting for transfers between devices  8.42 us (27%)
  starting transfers between devices  8.12 us (26%)
  local copies, waits for them, and re-layouts  2.55 us (8%)
  other arithmetic  0.87 us (3%)
  between operations  0.79 us (2%)
    ppermute x1, waiting for transfers between devices, paired(): edge = lax.ppermute(state[height - depth:], ('frame', 'row'), cross_both)  4.83 us
    pallas_call x1, Pallas kernels, paired(): pl.pallas_call(functools.partial(first_kernel, height), grid=(1,), out_sh...  3.43 us
    pallas_call x1, Pallas kernels, paired(): pl.pallas_call(functools.partial(second_kernel, height), grid=(1,), out_s...  3.12 us
    ppermute x1, starting transfers between devices, paired(): near_other = lax.ppermute(near_own, 'frame', swap_near)  2.98 us
    pallas_call x4, Pallas kernels, pack_weights(): pl.pallas_call(functools.partial(pack_kernel, phase, parts), out_shape=ja...  2.97 us
    ppermute x1, starting transfers between devices, paired(): incoming = lax.ppermute(state, 'frame', cross)  2.66 us
    unnamed x14, local copies, waits for them, and re-layouts  1.6 us
    ppermute x1, starting transfers between devices, paired(): far_other = lax.ppermute(edge, ('frame', 'row'), swap_both)  1.38 us
  transfers between devices with their start and end apart: 7, of which 4 were waited for; matrix products, arithmetic and copies ran while one was open for 0% of the time, Pallas kernels for 13%

commit v1 on v0

--- a/solution.py
+++ b/solution.py
@@ -153,11 +153,13 @@
     )(flags, *weights)
 
 
-def pack_phase(phase, flags, w_in, w_mid, w_out):
-    ch = w_mid.shape[-1]
-    outer = pack_weights(phase, ((0, 0), (0, ch)), flags, w_in)
+def pack_outer(phase, flags, w_in):
+    return pack_weights(phase, ((0, 0), (0, w_in.shape[-1])), flags, w_in)
+
+
+def pack_inner(phase, flags, outer, w_mid, w_out):
     flags, _ = lax.optimization_barrier((flags, outer))
-    return outer, pack_weights(phase, ((0, 0), (1, 0)), flags, w_mid, w_out)
+    return pack_weights(phase, ((0, 0), (1, 0)), flags, w_mid, w_out)
 
 
 def fields_of(refs):
@@ -177,7 +179,7 @@
                 ref[at] = v[p - lo] if keep is None else jnp.where(keep, ref[at].astype(jnp.float32), v[p - lo].astype(jnp.float32)).astype(ref.dtype)
 
 
-def first_kernel(height, flags, near_own, far_own, near_other, far_other, outer, inner, b_in, b_mid, b_out, state, result, *scratch):
+def first_kernel(height, flags, near_own, far_own, near_other, far_other, outer, inner, b_in, b_mid, b_out, state, edge, result, *scratch):
     flip, own_first = flags[0] == 1, flags[1] == 1
     bias = biases_of(flags[2], b_in, b_mid, b_out)
     w_f, w_s, w_m, w_o = outer.at[0], outer.at[1], inner.at[0], inner.at[1]
@@ -194,8 +196,10 @@
 
     def emit_second(lo, hi, a, b):
         for p in range(lo, hi):
-            state[2 * p] = a[p - lo]
-            state[2 * p + 1] = b[p - lo]
+            for i, v in ((2 * p, a[p - lo]), (2 * p + 1, b[p - lo])):
+                state[i] = v
+                if i >= height - edge.shape[0]:
+                    edge[i - (height - edge.shape[0])] = v
         store_canonical(result, flip, height, lo, hi, a, b, keep=own_first)
 
     def second_sums(lo, hi):
@@ -224,18 +228,17 @@
         sums[...] = conv_pairs(field, outer.at[0], 0, sums.shape[0])
 
 
-def second_kernel(height, flags, near, far, sums0, sums1, outer, inner, b_in, b_mid, b_out, result, *scratch):
+def second_kernel(height, flags, near_a, far_a, near_b, far_b, sums0, sums1, outer, inner, b_in, b_mid, b_out, result, *scratch):
     flip, own_first = flags[0] == 1, flags[1] == 1
     bias = biases_of(1 - flags[2], b_in, b_mid, b_out)
     w_s, w_m, w_o = outer.at[1], inner.at[0], inner.at[1]
     state, held, first0, middle0, first1, middle1 = fields = fields_of(scratch)
     for f in fields:
         f.clear()
-    depth = far.shape[0]
-    for i in range(height):
-        state.put_row(i, near[i])
-    for i in range(depth):
-        state.put_row(height + i, far[depth - 1 - i])
+    depth = far_a.shape[0]
+    for i in range(height + depth):
+        a, b, at = (near_a, near_b, i) if i < height else (far_a, far_b, height + depth - 1 - i)
+        state.put_row(i, jnp.where(own_first, a[at].astype(jnp.float32), b[at].astype(jnp.float32)))
     state.zero_row(height + depth)
 
     def emit_first(lo, hi, a, b):
@@ -243,20 +246,21 @@
         store_canonical(result, flip, height, lo, hi, a, b)
 
     def emit_second(lo, hi, a, b):
-        store_canonical(result, flip, height, lo, hi, a, b, keep=jnp.logical_not(own_first))
+        store_canonical(result, flip, height, lo, hi, a, b)
 
     n0, n1 = pair_sizes(height + 3), pair_sizes(height)
     middle0.zero_row(2 * n0[2])
-    first1.zero_row(2 * n1[0])
-    run(
-        frame_stages(lambda lo, hi: sums0[lo:hi] + conv_pairs(state, w_s, lo, hi), n0, first0, middle0, w_m, w_o, *bias, emit_first)
-        + frame_stages(lambda lo, hi: sums1[lo:hi] + conv_pairs(held, w_s, lo, hi), n1, first1, middle1, w_m, w_o, *bias, emit_second)
-    )
+    run(frame_stages(lambda lo, hi: sums0[lo:hi] + conv_pairs(state, w_s, lo, hi), n0, first0, middle0, w_m, w_o, *bias, emit_first))
+
+    @pl.when(own_first)
+    def _():
+        first1.zero_row(2 * n1[0])
+        run(frame_stages(lambda lo, hi: sums1[lo:hi] + conv_pairs(held, w_s, lo, hi), n1, first1, middle1, w_m, w_o, *bias, emit_second))
 
 
 VMEM = pl.BlockSpec(memory_space=pltpu.VMEM)
 SMEM = pl.BlockSpec(memory_space=pltpu.SMEM)
-LIMIT = 24 << 20
+LIMIT = 14 << 20
 
 
 def field_scratch(count, rows, cols, ch):
@@ -275,8 +279,16 @@
     swap_core = [(0, 1), (1, 0), (2, 3), (3, 2)]
     swap_column = [(0, 2), (2, 0), (1, 3), (3, 1)]
     swap_near = [(0, 1), (1, 0), (2, 3), (3, 2)]
-    cross = [(0, 2), (2, 0), (1, 3), (3, 1)]
-    cross_both = [(4 * f + r, 4 * (f ^ 2) + (r ^ 2)) for f in range(4) for r in range(4)]
+    outer_cross, inner_cross = (1, 3, 0, 2), (None, 2, 1, None)
+
+    def crossing(targets, mirror):
+        pairs = []
+        for f in range(4):
+            for r in range(4):
+                stays = targets[f] is None
+                pairs.append((4 * f + r, 4 * f + (r ^ 1) if stays else 4 * targets[f] + (r ^ mirror)))
+        return pairs
+
     swap_both = [(4 * f + r, 4 * (f ^ 1) + (r ^ 2)) for f in range(4) for r in range(4)]
 
     biases = (b_in, b_mid, b_out)
@@ -294,26 +306,31 @@
     bf16 = jnp.bfloat16
     cost = lambda rows: pl.CostEstimate(flops=rows * cols * ch * ch * 24, bytes_accessed=4 << 20, transcendentals=0)
     held_flags, _ = lax.optimization_barrier((flags, near_own))
-    packed = pack_phase(0, held_flags, w_in, w_mid, w_out)
-    state, early = pl.pallas_call(
+    outer = pack_outer(0, held_flags, w_in)
+    packed = outer, pack_inner(0, held_flags, outer, w_mid, w_out)
+    state, edge, early = pl.pallas_call(
         functools.partial(first_kernel, height),
         grid=(1,),
         out_shape=(
             jax.ShapeDtypeStruct((height, cols, ch), bf16),
+            jax.ShapeDtypeStruct((depth, cols, ch), bf16),
             jax.ShapeDtypeStruct((height, cols, ch), bf16),
         ),
         in_specs=[SMEM] + [VMEM] * 9,
-        out_specs=(VMEM, VMEM),
+        out_specs=(VMEM, VMEM, VMEM),
         scratch_shapes=field_scratch(7, rows, cols, ch),
         cost_estimate=cost(190),
         compiler_params=pltpu.CompilerParams(vmem_limit_bytes=LIMIT),
     )(flags, *frames, *packed, *biases)
 
-    incoming = lax.ppermute(state, "frame", cross)
-    edge = lax.ppermute(state[height - depth :], ("frame", "row"), cross_both)
+    handed = []
+    for targets in (outer_cross, inner_cross):
+        for rows_of, mirror in ((state, 0), (edge, 2)):
+            handed.append(lax.ppermute(rows_of, ("frame", "row"), crossing(targets, mirror)))
     held_flags, _ = lax.optimization_barrier((flags, state))
-    packed = pack_phase(1, held_flags, w_in, w_mid, w_out)
-    sums = pl.pallas_call(
+    outer = pack_outer(1, held_flags, w_in)
+    packed = outer, pack_inner(1, held_flags, outer, w_mid, w_out)
+    ahead = pl.pallas_call(
         functools.partial(ahead_kernel, height),
         grid=(1,),
         out_shape=tuple(jax.ShapeDtypeStruct((n, cols, 2 * ch), jnp.float32) for n in ((height + 6) // 2, (height + 3) // 2)),
@@ -322,17 +339,18 @@
         scratch_shapes=field_scratch(2, rows, cols, ch),
         cost_estimate=cost(42),
         compiler_params=pltpu.CompilerParams(vmem_limit_bytes=LIMIT),
-    )(flags, *frames, packed[0])
+    )
+    sums = ahead(flags, *frames, packed[0])
     later = pl.pallas_call(
         functools.partial(second_kernel, height),
         grid=(1,),
         out_shape=jax.ShapeDtypeStruct((height, cols, ch), bf16),
-        in_specs=[SMEM] + [VMEM] * 9,
+        in_specs=[SMEM] + [VMEM] * 11,
         out_specs=VMEM,
         scratch_shapes=field_scratch(6, rows, cols, ch),
         cost_estimate=cost(120),
         compiler_params=pltpu.CompilerParams(vmem_limit_bytes=LIMIT),
-    )(flags, incoming, edge, *sums, *packed, *biases)
+    )(flags, *handed, *sums, *packed, *biases)
 
     both = jnp.stack([early, later])
     kept = lax.dynamic_slice_in_dim(both, slab * core, slab, 1)

time: 31.7 us -> 32.1 us (1.013)
  starting transfers between devices: 8.12 us -> 9.73 us
  waiting for transfers between devices: 8.42 us -> 6.92 us
    ppermute x2 -> x4, starting transfers between devices: 2.95 us -> 4.56 us  [paired(): lax.ppermute(rows_of, ('frame', 'row'), crossing(targets, mirror))]
    ppermute x2 -> x4, waiting for transfers between devices: 4.83 us -> 3.33 us  [paired(): lax.ppermute(rows_of, ('frame', 'row'), crossing(targets, mirror))]
  transfers between devices with their start and end apart: 7 -> 9, of which waited for: 4 -> 4; matrix products, arithmetic and copies ran while one was open for 0% -> 0% of each run, Pallas kernels for 13% -> 13%
where the time goes in v1:
time: 32.1 us; the launch traced here: 31.8 us
  Pallas kernels  11 us (34%)
  starting transfers between devices  9.73 us (30%)
  waiting for transfers between devices  6.92 us (22%)
  local copies, waits for them, and re-layouts  2.55 us (8%)
  other arithmetic  0.87 us (3%)
  between operations  0.8 us (2%)
    ppermute x4, starting transfers between devices, paired(): lax.ppermute(rows_of, ('frame', 'row'), crossing(targets, mirror))  4.56 us
    pallas_call x1, Pallas kernels, paired(): pl.pallas_call(functools.partial(first_kernel, height), grid=(1,), out_sh...  3.38 us
    pallas_call x1, Pallas kernels, paired(): pl.pallas_call(functools.partial(second_kernel, height), grid=(1,), out_s...  3.35 us
    ppermute x4, waiting for transfers between devices, paired(): lax.ppermute(rows_of, ('frame', 'row'), crossing(targets, mirror))  3.33 us
    ppermute x1, starting transfers between devices, paired(): near_other = lax.ppermute(near_own, 'frame', swap_near)  2.98 us
    pallas_call x4, Pallas kernels, pack_weights(): pl.pallas_call(functools.partial(pack_kernel, phase, parts), out_shape=ja...  2.97 us
    unnamed x14, local copies, waits for them, and re-layouts  1.6 us
    ppermute x1, starting transfers between devices, paired(): far_other = lax.ppermute(edge, ('frame', 'row'), swap_both)  1.38 us
  transfers between devices with their start and end apart: 9, of which 4 were waited for; matrix products, arithmetic and copies ran while one was open for 0% of the time, Pallas kernels for 13%

profile of v1, /device:TPU:0, one launch (start us, length us, event | category | flops | bytes accessed | tf_op | source)
XLA Modules:
  0.0 31.8 jit_solution(7861644365567257968)
XLA Ops:
  0.7 0.9 %dynamic-slice_bitcast_fusion.1 = (bf16[8,32,128]{2,1,0:T(8,128)(2,1)S(1)}, bf16[8,32,128]{2,1,0:T(8,128)(2,1)S(1)}) fusion(bf16[2,1,8,32,128]{4,3,2,1,0:T(8,128)(2,1)} %param.7, s32[]{:T(128)S(6)} %select_n.80, s32[]{:T(128)S(6)} %select_n.81), kind=kLoop, calls=%fused_computation.12 | loop fusion | bytes 262152 | tf_op jit(solution)/shard_map/jit(dynamic_index_in_dim)/squeeze | solution.py:296
  1.6 0.6 %collective-permute-start = (bf16[8,32,128]{2,1,0:T(8,128)(2,1)S(1)}, bf16[8,32,128]{2,1,0:T(8,128)(2,1)S(1)}, u32[]{:S(2)}, u32[]{:S(2)}) collective-permute-start(bf16[8,32,128]{2,1,0:T(8,128)(2,1)S(1)} %get-tuple-element.27), channel_id=1, source_target_pairs={{0,1},{1,0},{2,3},{3,2},{4,5},{5,4},{6,7},{7,6},{8,9},{9,8},{10,11... | collective-permute-start | bytes 196616 | tf_op jit(solution)/shard_map/ppermute | solution.py:297
  2.2 0.9 %collective-permute-done = bf16[8,32,128]{2,1,0:T(8,128)(2,1)S(1)} collective-permute-done((bf16[8,32,128]{2,1,0:T(8,128)(2,1)S(1)}, bf16[8,32,128]{2,1,0:T(8,128)(2,1)S(1)}, u32[]{:S(2)}, u32[]{:S(2)}) %collective-permute-start) | collective-permute-done | bytes 65568 | tf_op jit(solution)/shard_map/ppermute | solution.py:297
  3.1 3.0 %collective-permute-start.2 = (bf16[16,32,128]{2,1,0:T(8,128)(2,1)S(1)}, bf16[16,32,128]{2,1,0:T(8,128)(2,1)S(1)}, u32[]{:S(2)}, u32[]{:S(2)}) collective-permute-start(bf16[16,32,128]{2,1,0:T(8,128)(2,1)S(1)} %maximum_select_fusion.1.near_own), channel_id=1, source_target_pairs={{0,4},{4,0},{8,12},{12,8},{1,5},{5,1},{9,13},{13,9},{2,6},{6,2},{1... | collective-permute-start | bytes 393224 | tf_op jit(solution)/shard_map/ppermute | solution.py:300
  6.1 1.4 %collective-permute-start.3 = (bf16[6,32,128]{2,1,0:T(8,128)(2,1)S(1)}, bf16[6,32,128]{2,1,0:T(8,128)(2,1)S(1)}, u32[]{:S(2)}, u32[]{:S(2)}) collective-permute-start(bf16[6,32,128]{2,1,0:T(8,128)(2,1)S(1)} %constant_dynamic-slice_fusion), channel_id=1, source_target_pairs={{0,6},{1,7},{2,4},{3,5},{4,2},{5,3},{6,0},{7,1},{8,14},{9,15},{10,... | collective-permute-start | bytes 147464 | tf_op jit(solution)/shard_map/ppermute | solution.py:302
  7.5 0.2 collective-permute-start.1
  7.6 0.1 pad_add_fusion.flags
  7.7 1.3 %copy-done = bf16[2,3,3,256,128]{4,3,2,1,0:T(8,128)(2,1)S(1)} copy-done((bf16[2,3,3,256,128]{4,3,2,1,0:T(8,128)(2,1)S(1)}, bf16[2,3,3,256,128]{4,3,2,1,0:T(8,128)(2,1)}, u32[]{:S(2)}) %copy-start) | copy-done | bytes 1179672
  9.0 0.7 %shard_map.86.outer = bf16[2,1536,256]{2,1,0:T(8,128)(2,1)S(1)} custom-call(s32[3]{0:T(128)S(1)} %pad_add_fusion.flags, bf16[2,3,3,256,128]{4,3,2,1,0:T(8,128)(2,1)S(1)} %copy-done), custom_call_target="tpu_custom_call" | custom-call | bytes 8388608 | tf_op jit(solution)/shard_map/pallas_call | solution.py:146
  9.7 0.3 copy-done.3
  10.1 0.7 %shard_map.87.inner = bf16[2,1536,256]{2,1,0:T(8,128)(2,1)S(1)} custom-call(s32[3]{0:T(128)S(1)} %pad_add_fusion.flags, bf16[2,3,3,128,128]{4,3,2,1,0:T(8,128)(2,1)S(1)} %copy-done.2, bf16[2,3,3,128,128]{4,3,2,1,0:T(8,128)(2,1)S(1)} %copy-done.3), custom_call_target="tpu_custom_call" | custom-call | bytes 8388608 | tf_op jit(solution)/shard_map/pallas_call | solution.py:146
  10.8 1.3 %collective-permute-done.3.far_other = bf16[6,32,128]{2,1,0:T(8,128)(2,1)S(1)} collective-permute-done((bf16[6,32,128]{2,1,0:T(8,128)(2,1)S(1)}, bf16[6,32,128]{2,1,0:T(8,128)(2,1)S(1)}, u32[]{:S(2)}, u32[]{:S(2)}) %collective-permute-start.3) | collective-permute-done | bytes 49184 | tf_op jit(solution)/shard_map/ppermute | solution.py:302
  12.2 3.4 %shard_map.88 = (bf16[16,32,128]{2,1,0:T(8,128)(2,1)S(1)}, bf16[6,32,128]{2,1,0:T(8,128)(2,1)S(1)}, bf16[16,32,128]{2,1,0:T(8,128)(2,1)S(1)}) custom-call(s32[3]{0:T(128)S(1)} %pad_add_fusion.flags, bf16[16,32,128]{2,1,0:T(8,128)(2,1)S(1)} %maximum_select_fusion.1.near_own, bf16[6,32,128]{2,1,0:T(8,128)(2,1)S(1)} %collective-permute-done.1.far_own, ...), custom_call_target="tpu_custom_call" | custom-call | flops 2390753280 | bytes 4194304 | tf_op jit(solution)/shard_map/pallas_call | solution.py:311
  15.6 0.1 collective-permute-start.6
  15.7 3.1 %collective-permute-start.4 = (bf16[16,32,128]{2,1,0:T(8,128)(2,1)S(1)}, bf16[16,32,128]{2,1,0:T(8,128)(2,1)S(1)}, u32[]{:S(2)}, u32[]{:S(2)}) collective-permute-start(bf16[16,32,128]{2,1,0:T(8,128)(2,1)S(1)} %get-tuple-element.14), channel_id=1, source_target_pairs={{0,4},{1,5},{2,6},{3,7},{4,12},{5,13},{6,14},{7,15},{8,0},{9,1},{1... | collective-permute-start | bytes 393224 | tf_op jit(solution)/shard_map/ppermute | solution.py:329
  18.8 1.3 %collective-permute-start.5 = (bf16[6,32,128]{2,1,0:T(8,128)(2,1)S(1)}, bf16[6,32,128]{2,1,0:T(8,128)(2,1)S(1)}, u32[]{:S(2)}, u32[]{:S(2)}) collective-permute-start(bf16[6,32,128]{2,1,0:T(8,128)(2,1)S(1)} %get-tuple-element.15), channel_id=1, source_target_pairs={{0,6},{1,7},{2,4},{3,5},{4,14},{5,15},{6,12},{7,13},{8,2},{9,3},{1... | collective-permute-start | bytes 147464 | tf_op jit(solution)/shard_map/ppermute | solution.py:329
  20.2 0.7 %shard_map.89.outer = bf16[2,1536,256]{2,1,0:T(8,128)(2,1)S(1)} custom-call(s32[3]{0:T(128)S(1)} %pad_add_fusion.flags, bf16[2,3,3,256,128]{4,3,2,1,0:T(8,128)(2,1)S(1)} %copy-done.1), custom_call_target="tpu_custom_call" | custom-call | bytes 8388608 | tf_op jit(solution)/shard_map/pallas_call | solution.py:146
  20.9 0.7 %shard_map.91.inner = bf16[2,1536,256]{2,1,0:T(8,128)(2,1)S(1)} custom-call(s32[3]{0:T(128)S(1)} %pad_add_fusion.flags, bf16[2,3,3,128,128]{4,3,2,1,0:T(8,128)(2,1)S(1)} %copy-done.2, bf16[2,3,3,128,128]{4,3,2,1,0:T(8,128)(2,1)S(1)} %copy-done.3), custom_call_target="tpu_custom_call" | custom-call | bytes 8388608 | tf_op jit(solution)/shard_map/pallas_call | solution.py:146
  21.7 1.3 %shard_map.90 = (f32[11,32,256]{2,1,0:T(8,128)S(1)}, f32[9,32,256]{2,1,0:T(8,128)S(1)}) custom-call(s32[3]{0:T(128)S(1)} %pad_add_fusion.flags, bf16[16,32,128]{2,1,0:T(8,128)(2,1)S(1)} %maximum_select_fusion.1.near_own, bf16[6,32,128]{2,1,0:T(8,128)(2,1)S(1)} %collective-permute-done.1.far_own, bf16[16,32,128]{2,1,0:T(8,128)(2,1)S(1)} %collective-permute-done.2.near_other, ...), custom_call_target="tpu_custom_call" | custom-call | flops 528482304 | bytes 4194304 | tf_op jit(solution)/shard_map/pallas_call | solution.py:343
  22.9 3.3 %collective-permute-done.5.far_a = bf16[6,32,128]{2,1,0:T(8,128)(2,1)S(1)} collective-permute-done((bf16[6,32,128]{2,1,0:T(8,128)(2,1)S(1)}, bf16[6,32,128]{2,1,0:T(8,128)(2,1)S(1)}, u32[]{:S(2)}, u32[]{:S(2)}) %collective-permute-start.5) | collective-permute-done | bytes 49184 | tf_op jit(solution)/shard_map/ppermute | solution.py:329
  26.3 3.4 %shard_map.92 = bf16[16,32,128]{2,1,0:T(8,128)(2,1)S(1)} custom-call(s32[3]{0:T(128)S(1)} %pad_add_fusion.flags, bf16[16,32,128]{2,1,0:T(8,128)(2,1)S(1)} %collective-permute-done.4.near_a, bf16[6,32,128]{2,1,0:T(8,128)(2,1)S(1)} %collective-permute-done.5.far_a, bf16[16,32,128]{2,1,0:T(8,128)(2,1)S(1)} %collective-permute-done.6.near_b, ...), custom_call_target="tpu_custom_call" | custom-call | flops 1509949440 | bytes 4194304 | tf_op jit(solution)/shard_map/pallas_call | solution.py:344
  29.7 0.1 collective-permute-start.8
  29.8 1.3 %collective-permute-done.8 = bf16[2,8,32,128]{3,2,1,0:T(8,128)(2,1)S(1)} collective-permute-done((bf16[2,8,32,128]{3,2,1,0:T(8,128)(2,1)S(1)}, bf16[2,8,32,128]{3,2,1,0:T(8,128)(2,1)S(1)}, u32[]{:S(2)}, u32[]{:S(2)}) %collective-permute-start.8) | collective-permute-done | bytes 131104 | tf_op jit(solution)/shard_map/ppermute | solution.py:357
  31.1 0.7 %select_bitcast_fusion = (bf16[2,1,8,32,128]{4,3,2,1,0:T(8,128)(2,1)}, bf16[2,1,8,32,128]{4,3,2,1,0:T(8,128)(2,1)}) fusion(pred[]{:T(512)S(6)} %eq.16, bf16[2,2,8,32,128]{4,3,2,0,1:T(8,128)(2,1)S(1)} %maximum_select_fusion), kind=kLoop, calls=%fused_computation.9 | loop fusion | flops 131072 | bytes 524289
  (22 shorter events, 0.2 us)
Async XLA Ops:
  0.7 9.1 %copy-start.2 = (bf16[2,3,3,128,128]{4,3,2,1,0:T(8,128)(2,1)S(1)}, bf16[2,3,3,128,128]{4,3,2,1,0:T(8,128)(2,1)}, u32[]{:S(2)}) copy-start(bf16[2,3,3,128,128]{4,3,2,1,0:T(8,128)(2,1)} %refs_0_.7) | copy-start | bytes 1769476
  1.6 1.5 %collective-permute-start = (bf16[8,32,128]{2,1,0:T(8,128)(2,1)S(1)}, bf16[8,32,128]{2,1,0:T(8,128)(2,1)S(1)}, u32[]{:S(2)}, u32[]{:S(2)}) collective-permute-start(bf16[8,32,128]{2,1,0:T(8,128)(2,1)S(1)} %get-tuple-element.27), channel_id=1, source_target_pairs={{0,1},{1,0},{2,3},{3,2},{4,5},{5,4},{6,7},{7,6},{8,9},{9,8},{10,11... | collective-permute-start | bytes 196616 | tf_op jit(solution)/shard_map/ppermute | solution.py:297
  3.1 9.1 %collective-permute-start.2 = (bf16[16,32,128]{2,1,0:T(8,128)(2,1)S(1)}, bf16[16,32,128]{2,1,0:T(8,128)(2,1)S(1)}, u32[]{:S(2)}, u32[]{:S(2)}) collective-permute-start(bf16[16,32,128]{2,1,0:T(8,128)(2,1)S(1)} %maximum_select_fusion.1.near_own), channel_id=1, source_target_pairs={{0,4},{4,0},{8,12},{12,8},{1,5},{5,1},{9,13},{13,9},{2,6},{6,2},{1... | collective-permute-start | bytes 393224 | tf_op jit(solution)/shard_map/ppermute | solution.py:300
  6.1 6.1 %collective-permute-start.3 = (bf16[6,32,128]{2,1,0:T(8,128)(2,1)S(1)}, bf16[6,32,128]{2,1,0:T(8,128)(2,1)S(1)}, u32[]{:S(2)}, u32[]{:S(2)}) collective-permute-start(bf16[6,32,128]{2,1,0:T(8,128)(2,1)S(1)} %constant_dynamic-slice_fusion), channel_id=1, source_target_pairs={{0,6},{1,7},{2,4},{3,5},{4,2},{5,3},{6,0},{7,1},{8,14},{9,15},{10,... | collective-permute-start | bytes 147464 | tf_op jit(solution)/shard_map/ppermute | solution.py:302
  7.5 4.7 %collective-permute-start.1 = (bf16[6,32,128]{2,1,0:T(8,128)(2,1)S(1)}, bf16[6,32,128]{2,1,0:T(8,128)(2,1)S(1)}, u32[]{:S(2)}, u32[]{:S(2)}) collective-permute-start(bf16[6,32,128]{2,1,0:T(8,128)(2,1)S(1)} %constant_dynamic-slice_fusion), channel_id=1, source_target_pairs={{0,2},{2,0},{1,3},{3,1},{4,6},{6,4},{5,7},{7,5},{8,10},{10,8},{9,1... | collective-permute-start | bytes 147464 | tf_op jit(solution)/shard_map/ppermute | solution.py:301
  7.7 1.3 %copy-start = (bf16[2,3,3,256,128]{4,3,2,1,0:T(8,128)(2,1)S(1)}, bf16[2,3,3,256,128]{4,3,2,1,0:T(8,128)(2,1)}, u32[]{:S(2)}) copy-start(bf16[2,3,3,256,128]{4,3,2,1,0:T(8,128)(2,1)} %refs_0_.6) | copy-start | bytes 3538948
  9.0 1.1 %copy-start.3 = (bf16[2,3,3,128,128]{4,3,2,1,0:T(8,128)(2,1)S(1)}, bf16[2,3,3,128,128]{4,3,2,1,0:T(8,128)(2,1)}, u32[]{:S(2)}) copy-start(bf16[2,3,3,128,128]{4,3,2,1,0:T(8,128)(2,1)} %refs_1_.3) | copy-start | bytes 1769476
  10.0 2.1 %copy-start.4 = (f32[2,128]{1,0:T(2,128)S(1)}, f32[2,128]{1,0:T(2,128)}, u32[]{:S(2)}) copy-start(f32[2,128]{1,0:T(2,128)} %b_in.3) | copy-start | bytes 3076
  10.0 2.1 %copy-start.5 = (f32[2,128]{1,0:T(2,128)S(1)}, f32[2,128]{1,0:T(2,128)}, u32[]{:S(2)}) copy-start(f32[2,128]{1,0:T(2,128)} %b_mid.3) | copy-start | bytes 3076
  10.1 2.1 %copy-start.6 = (f32[2,128]{1,0:T(2,128)S(1)}, f32[2,128]{1,0:T(2,128)}, u32[]{:S(2)}) copy-start(f32[2,128]{1,0:T(2,128)} %b_out.3) | copy-start | bytes 3076
  10.8 9.4 %copy-start.1 = (bf16[2,3,3,256,128]{4,3,2,1,0:T(8,128)(2,1)S(1)}, bf16[2,3,3,256,128]{4,3,2,1,0:T(8,128)(2,1)}, u32[]{:S(2)}) copy-start(bf16[2,3,3,256,128]{4,3,2,1,0:T(8,128)(2,1)} %refs_0_.6) | copy-start | bytes 3538948
  15.6 10.7 %collective-permute-start.6 = (bf16[16,32,128]{2,1,0:T(8,128)(2,1)S(1)}, bf16[16,32,128]{2,1,0:T(8,128)(2,1)S(1)}, u32[]{:S(2)}, u32[]{:S(2)}) collective-permute-start(bf16[16,32,128]{2,1,0:T(8,128)(2,1)S(1)} %get-tuple-element.14), channel_id=1, source_target_pairs={{0,1},{1,0},{2,3},{3,2},{4,8},{5,9},{6,10},{7,11},{8,4},{9,5},{10,... | collective-permute-start | bytes 393224 | tf_op jit(solution)/shard_map/ppermute | solution.py:329
  15.7 10.6 %collective-permute-start.4 = (bf16[16,32,128]{2,1,0:T(8,128)(2,1)S(1)}, bf16[16,32,128]{2,1,0:T(8,128)(2,1)S(1)}, u32[]{:S(2)}, u32[]{:S(2)}) collective-permute-start(bf16[16,32,128]{2,1,0:T(8,128)(2,1)S(1)} %get-tuple-element.14), channel_id=1, source_target_pairs={{0,4},{1,5},{2,6},{3,7},{4,12},{5,13},{6,14},{7,15},{8,0},{9,1},{1... | collective-permute-start | bytes 393224 | tf_op jit(solution)/shard_map/ppermute | solution.py:329
  18.8 4.1 %collective-permute-start.7 = (bf16[6,32,128]{2,1,0:T(8,128)(2,1)S(1)}, bf16[6,32,128]{2,1,0:T(8,128)(2,1)S(1)}, u32[]{:S(2)}, u32[]{:S(2)}) collective-permute-start(bf16[6,32,128]{2,1,0:T(8,128)(2,1)S(1)} %get-tuple-element.15), channel_id=1, source_target_pairs={{0,1},{1,0},{2,3},{3,2},{4,10},{5,11},{6,8},{7,9},{8,6},{9,7},{10,... | collective-permute-start | bytes 147464 | tf_op jit(solution)/shard_map/ppermute | solution.py:329
  18.8 7.5 %collective-permute-start.5 = (bf16[6,32,128]{2,1,0:T(8,128)(2,1)S(1)}, bf16[6,32,128]{2,1,0:T(8,128)(2,1)S(1)}, u32[]{:S(2)}, u32[]{:S(2)}) collective-permute-start(bf16[6,32,128]{2,1,0:T(8,128)(2,1)S(1)} %get-tuple-element.15), channel_id=1, source_target_pairs={{0,6},{1,7},{2,4},{3,5},{4,14},{5,15},{6,12},{7,13},{8,2},{9,3},{1... | collective-permute-start | bytes 147464 | tf_op jit(solution)/shard_map/ppermute | solution.py:329
  29.7 1.4 %collective-permute-start.8 = (bf16[2,8,32,128]{3,2,1,0:T(8,128)(2,1)S(1)}, bf16[2,8,32,128]{3,2,1,0:T(8,128)(2,1)S(1)}, u32[]{:S(2)}, u32[]{:S(2)}) collective-permute-start(bf16[2,8,32,128]{3,2,1,0:T(8,128)(2,1)S(1)} %get-tuple-element.25), channel_id=1, source_target_pairs={{0,1},{1,0},{2,3},{3,2},{4,5},{5,4},{6,7},{7,6},{8,9},{9,8},{10,11... | collective-permute-start | bytes 393224 | tf_op jit(solution)/shard_map/ppermute | solution.py:357

commit v2 on v1

--- a/solution.py
+++ b/solution.py
@@ -12,34 +12,38 @@
     return 0.5 * v * (1.0 + lax.erf(v * 0.7071067811865476))
 
 
-def widen(rows):
-    cols = rows.shape[1]
-    col = lax.broadcasted_iota(jnp.int32, rows.shape, 1)
-    left = jnp.where(col == 0, 0.0, pltpu.roll(rows, 1, 1))
-    right = jnp.where(col == cols - 1, 0.0, pltpu.roll(rows, cols - 1, 1))
-    return jnp.concatenate([left, rows, right], axis=-1).astype(jnp.bfloat16)
-
-
 class Field:
-    def __init__(self, even, odd):
+    def __init__(self, even, odd, wide_even, wide_odd):
         self.even, self.odd = even, odd
+        self.wide = wide_even, wide_odd
 
     def clear(self):
         self.odd[0] = jnp.zeros(self.odd.shape[1:], self.odd.dtype)
+        for wide in self.wide:
+            n, cols, ch = wide.shape
+            wide[:, :8, :] = jnp.zeros((n, 8, ch), wide.dtype)
+            wide[:, cols - 8 :, :] = jnp.zeros((n, 8, ch), wide.dtype)
+
+    def widened(self, k, lo, hi, rows):
+        wide = self.wide[k]
+        cols = rows.shape[1]
+        wide[lo:hi, 8 : 8 + cols, :] = rows
+        left, right = wide[lo:hi, 7 : 7 + cols, :], wide[lo:hi, 9 : 9 + cols, :]
+        return jnp.concatenate([left, rows, right], axis=-1).astype(jnp.bfloat16)
 
     def zero_row(self, row):
         self.even[row // 2] = jnp.zeros(self.even.shape[1:], self.even.dtype)
 
     def put_row(self, row, value):
-        wide = widen(value.astype(jnp.float32)[None])[0]
+        wide = self.widened(row % 2, row // 2, row // 2 + 1, value.astype(jnp.float32)[None])[0]
         if row % 2 == 0:
             self.even[row // 2] = wide
         else:
             self.odd[row // 2 + 1] = wide
 
     def put_pairs(self, lo, hi, first, second):
-        self.even[lo:hi] = widen(first)
-        self.odd[lo + 1 : hi + 1] = widen(second)
+        self.even[lo:hi] = self.widened(0, lo, hi, first)
+        self.odd[lo + 1 : hi + 1] = self.widened(1, lo, hi, second)
 
     def patches(self, lo, hi):
         n = hi - lo
@@ -65,10 +69,7 @@
     return acc[:, :, :ch] + bias, acc[:, :, ch:] + bias
 
 
-SPLIT = 7
-
-
-def run(stages):
+def run(stages, split):
     waiting = []
 
     def finish_to(count):
@@ -77,7 +78,7 @@
             done[0](*done[1:])
 
     for s, (pairs, sums, finish) in enumerate(stages):
-        edge = min(max(SPLIT - s, 0), pairs)
+        edge = min(max(split - s, 0), pairs)
         if edge == 0 or edge == pairs:
             finish_to(0)
             waiting.append((finish, 0, pairs, sums(0, pairs)))
@@ -163,7 +164,7 @@
 
 
 def fields_of(refs):
-    return [Field(refs[2 * i], refs[2 * i + 1]) for i in range(len(refs) // 2)]
+    return [Field(*refs[4 * i : 4 * i + 4]) for i in range(len(refs) // 4)]
 
 
 def biases_of(direction, *refs):
@@ -211,7 +212,8 @@
     first1.zero_row(2 * n1[0])
     run(
         frame_stages(lambda lo, hi: conv_pairs(frame0, w_f, lo, hi), n0, first0, middle0, w_m, w_o, *bias, emit_first)
-        + frame_stages(second_sums, n1, first1, middle1, w_m, w_o, *bias, emit_second)
+        + frame_stages(second_sums, n1, first1, middle1, w_m, w_o, *bias, emit_second),
+        8,
     )
 
 
@@ -250,12 +252,12 @@
 
     n0, n1 = pair_sizes(height + 3), pair_sizes(height)
     middle0.zero_row(2 * n0[2])
-    run(frame_stages(lambda lo, hi: sums0[lo:hi] + conv_pairs(state, w_s, lo, hi), n0, first0, middle0, w_m, w_o, *bias, emit_first))
+    run(frame_stages(lambda lo, hi: sums0[lo:hi] + conv_pairs(state, w_s, lo, hi), n0, first0, middle0, w_m, w_o, *bias, emit_first), 7)
 
     @pl.when(own_first)
     def _():
         first1.zero_row(2 * n1[0])
-        run(frame_stages(lambda lo, hi: sums1[lo:hi] + conv_pairs(held, w_s, lo, hi), n1, first1, middle1, w_m, w_o, *bias, emit_second))
+        run(frame_stages(lambda lo, hi: sums1[lo:hi] + conv_pairs(held, w_s, lo, hi), n1, first1, middle1, w_m, w_o, *bias, emit_second), 7)
 
 
 VMEM = pl.BlockSpec(memory_space=pltpu.VMEM)
@@ -264,7 +266,9 @@
 
 
 def field_scratch(count, rows, cols, ch):
-    return [pltpu.VMEM((rows // 2 + 1, cols, 3 * ch), jnp.bfloat16) for _ in range(2 * count)]
+    wide = pltpu.VMEM((rows // 2 + 1, cols, 3 * ch), jnp.bfloat16)
+    padded = pltpu.VMEM((rows // 2, cols + 16, ch), jnp.float32)
+    return [wide, wide, padded, padded] * count
 
 
 def paired(features, w_in, b_in, w_mid, b_mid, w_out, b_out):

time: 32.1 us -> 32.1 us (level)
  no operation moved by 1% of the time
where the time goes in v2:
time: 32.1 us; the launch traced here: 31.9 us
  Pallas kernels  11.1 us (35%)
  starting transfers between devices  9.73 us (30%)
  waiting for transfers between devices  6.87 us (21%)
  local copies, waits for them, and re-layouts  2.55 us (8%)
  other arithmetic  0.87 us (3%)
  between operations  0.81 us (3%)
    ppermute x4, starting transfers between devices, paired(): lax.ppermute(rows_of, ('frame', 'row'), crossing(targets, mirror))  4.56 us
    pallas_call x1, Pallas kernels, paired(): pl.pallas_call(functools.partial(first_kernel, height), grid=(1,), out_sh...  3.41 us
    pallas_call x1, Pallas kernels, paired(): pl.pallas_call(functools.partial(second_kernel, height), grid=(1,), out_s...  3.36 us
    ppermute x4, waiting for transfers between devices, paired(): lax.ppermute(rows_of, ('frame', 'row'), crossing(targets, mirror))  3.28 us
    ppermute x1, starting transfers between devices, paired(): near_other = lax.ppermute(near_own, 'frame', swap_near)  2.98 us
    pallas_call x4, Pallas kernels, pack_weights(): pl.pallas_call(functools.partial(pack_kernel, phase, parts), out_shape=ja...  2.97 us
    unnamed x14, local copies, waits for them, and re-layouts  1.6 us
    ppermute x1, starting transfers between devices, paired(): far_other = lax.ppermute(edge, ('frame', 'row'), swap_both)  1.38 us
  transfers between devices with their start and end apart: 9, of which 4 were waited for; matrix products, arithmetic and copies ran while one was open for 0% of the time, Pallas kernels for 13%

profile of v2, /device:TPU:0, one launch (start us, length us, event | category | flops | bytes accessed | tf_op | source)
XLA Modules:
  0.0 31.9 jit_solution(18128665457788130480)
XLA Ops:
  0.7 0.9 %dynamic-slice_bitcast_fusion.1 = (bf16[8,32,128]{2,1,0:T(8,128)(2,1)S(1)}, bf16[8,32,128]{2,1,0:T(8,128)(2,1)S(1)}) fusion(bf16[2,1,8,32,128]{4,3,2,1,0:T(8,128)(2,1)} %param.7, s32[]{:T(128)S(6)} %select_n.80, s32[]{:T(128)S(6)} %select_n.81), kind=kLoop, calls=%fused_computation.12 | loop fusion | bytes 262152 | tf_op jit(solution)/shard_map/jit(dynamic_index_in_dim)/squeeze | solution.py:300
  1.6 0.6 %collective-permute-start = (bf16[8,32,128]{2,1,0:T(8,128)(2,1)S(1)}, bf16[8,32,128]{2,1,0:T(8,128)(2,1)S(1)}, u32[]{:S(2)}, u32[]{:S(2)}) collective-permute-start(bf16[8,32,128]{2,1,0:T(8,128)(2,1)S(1)} %get-tuple-element.27), channel_id=1, source_target_pairs={{0,1},{1,0},{2,3},{3,2},{4,5},{5,4},{6,7},{7,6},{8,9},{9,8},{10,11... | collective-permute-start | bytes 196616 | tf_op jit(solution)/shard_map/ppermute | solution.py:301
  2.2 0.9 %collective-permute-done = bf16[8,32,128]{2,1,0:T(8,128)(2,1)S(1)} collective-permute-done((bf16[8,32,128]{2,1,0:T(8,128)(2,1)S(1)}, bf16[8,32,128]{2,1,0:T(8,128)(2,1)S(1)}, u32[]{:S(2)}, u32[]{:S(2)}) %collective-permute-start) | collective-permute-done | bytes 65568 | tf_op jit(solution)/shard_map/ppermute | solution.py:301
  3.1 3.0 %collective-permute-start.2 = (bf16[16,32,128]{2,1,0:T(8,128)(2,1)S(1)}, bf16[16,32,128]{2,1,0:T(8,128)(2,1)S(1)}, u32[]{:S(2)}, u32[]{:S(2)}) collective-permute-start(bf16[16,32,128]{2,1,0:T(8,128)(2,1)S(1)} %maximum_select_fusion.1.near_own), channel_id=1, source_target_pairs={{0,4},{4,0},{8,12},{12,8},{1,5},{5,1},{9,13},{13,9},{2,6},{6,2},{1... | collective-permute-start | bytes 393224 | tf_op jit(solution)/shard_map/ppermute | solution.py:304
  6.1 1.4 %collective-permute-start.3 = (bf16[6,32,128]{2,1,0:T(8,128)(2,1)S(1)}, bf16[6,32,128]{2,1,0:T(8,128)(2,1)S(1)}, u32[]{:S(2)}, u32[]{:S(2)}) collective-permute-start(bf16[6,32,128]{2,1,0:T(8,128)(2,1)S(1)} %constant_dynamic-slice_fusion), channel_id=1, source_target_pairs={{0,6},{1,7},{2,4},{3,5},{4,2},{5,3},{6,0},{7,1},{8,14},{9,15},{10,... | collective-permute-start | bytes 147464 | tf_op jit(solution)/shard_map/ppermute | solution.py:306
  7.5 0.2 collective-permute-start.1
  7.6 0.1 pad_add_fusion.flags
  7.7 1.3 %copy-done = bf16[2,3,3,256,128]{4,3,2,1,0:T(8,128)(2,1)S(1)} copy-done((bf16[2,3,3,256,128]{4,3,2,1,0:T(8,128)(2,1)S(1)}, bf16[2,3,3,256,128]{4,3,2,1,0:T(8,128)(2,1)}, u32[]{:S(2)}) %copy-start) | copy-done | bytes 1179672
  9.0 0.7 %shard_map.86.outer = bf16[2,1536,256]{2,1,0:T(8,128)(2,1)S(1)} custom-call(s32[3]{0:T(128)S(1)} %pad_add_fusion.flags, bf16[2,3,3,256,128]{4,3,2,1,0:T(8,128)(2,1)S(1)} %copy-done), custom_call_target="tpu_custom_call" | custom-call | bytes 8388608 | tf_op jit(solution)/shard_map/pallas_call | solution.py:147
  9.7 0.3 copy-done.3
  10.1 0.7 %shard_map.87.inner = bf16[2,1536,256]{2,1,0:T(8,128)(2,1)S(1)} custom-call(s32[3]{0:T(128)S(1)} %pad_add_fusion.flags, bf16[2,3,3,128,128]{4,3,2,1,0:T(8,128)(2,1)S(1)} %copy-done.2, bf16[2,3,3,128,128]{4,3,2,1,0:T(8,128)(2,1)S(1)} %copy-done.3), custom_call_target="tpu_custom_call" | custom-call | bytes 8388608 | tf_op jit(solution)/shard_map/pallas_call | solution.py:147
  10.8 1.3 %collective-permute-done.3.far_other = bf16[6,32,128]{2,1,0:T(8,128)(2,1)S(1)} collective-permute-done((bf16[6,32,128]{2,1,0:T(8,128)(2,1)S(1)}, bf16[6,32,128]{2,1,0:T(8,128)(2,1)S(1)}, u32[]{:S(2)}, u32[]{:S(2)}) %collective-permute-start.3) | collective-permute-done | bytes 49184 | tf_op jit(solution)/shard_map/ppermute | solution.py:306
  12.2 3.4 %shard_map.88 = (bf16[16,32,128]{2,1,0:T(8,128)(2,1)S(1)}, bf16[6,32,128]{2,1,0:T(8,128)(2,1)S(1)}, bf16[16,32,128]{2,1,0:T(8,128)(2,1)S(1)}) custom-call(s32[3]{0:T(128)S(1)} %pad_add_fusion.flags, bf16[16,32,128]{2,1,0:T(8,128)(2,1)S(1)} %maximum_select_fusion.1.near_own, bf16[6,32,128]{2,1,0:T(8,128)(2,1)S(1)} %collective-permute-done.1.far_own, ...), custom_call_target="tpu_custom_call" | custom-call | flops 2390753280 | bytes 4194304 | tf_op jit(solution)/shard_map/pallas_call | solution.py:315
  15.6 0.1 collective-permute-start.6
  15.7 3.1 %collective-permute-start.4 = (bf16[16,32,128]{2,1,0:T(8,128)(2,1)S(1)}, bf16[16,32,128]{2,1,0:T(8,128)(2,1)S(1)}, u32[]{:S(2)}, u32[]{:S(2)}) collective-permute-start(bf16[16,32,128]{2,1,0:T(8,128)(2,1)S(1)} %get-tuple-element.14), channel_id=1, source_target_pairs={{0,4},{1,5},{2,6},{3,7},{4,12},{5,13},{6,14},{7,15},{8,0},{9,1},{1... | collective-permute-start | bytes 393224 | tf_op jit(solution)/shard_map/ppermute | solution.py:333
  18.8 1.3 %collective-permute-start.5 = (bf16[6,32,128]{2,1,0:T(8,128)(2,1)S(1)}, bf16[6,32,128]{2,1,0:T(8,128)(2,1)S(1)}, u32[]{:S(2)}, u32[]{:S(2)}) collective-permute-start(bf16[6,32,128]{2,1,0:T(8,128)(2,1)S(1)} %get-tuple-element.15), channel_id=1, source_target_pairs={{0,6},{1,7},{2,4},{3,5},{4,14},{5,15},{6,12},{7,13},{8,2},{9,3},{1... | collective-permute-start | bytes 147464 | tf_op jit(solution)/shard_map/ppermute | solution.py:333
  20.2 0.7 %shard_map.89.outer = bf16[2,1536,256]{2,1,0:T(8,128)(2,1)S(1)} custom-call(s32[3]{0:T(128)S(1)} %pad_add_fusion.flags, bf16[2,3,3,256,128]{4,3,2,1,0:T(8,128)(2,1)S(1)} %copy-done.1), custom_call_target="tpu_custom_call" | custom-call | bytes 8388608 | tf_op jit(solution)/shard_map/pallas_call | solution.py:147
  20.9 0.7 %shard_map.91.inner = bf16[2,1536,256]{2,1,0:T(8,128)(2,1)S(1)} custom-call(s32[3]{0:T(128)S(1)} %pad_add_fusion.flags, bf16[2,3,3,128,128]{4,3,2,1,0:T(8,128)(2,1)S(1)} %copy-done.2, bf16[2,3,3,128,128]{4,3,2,1,0:T(8,128)(2,1)S(1)} %copy-done.3), custom_call_target="tpu_custom_call" | custom-call | bytes 8388608 | tf_op jit(solution)/shard_map/pallas_call | solution.py:147
  21.7 1.3 %shard_map.90 = (f32[11,32,256]{2,1,0:T(8,128)S(1)}, f32[9,32,256]{2,1,0:T(8,128)S(1)}) custom-call(s32[3]{0:T(128)S(1)} %pad_add_fusion.flags, bf16[16,32,128]{2,1,0:T(8,128)(2,1)S(1)} %maximum_select_fusion.1.near_own, bf16[6,32,128]{2,1,0:T(8,128)(2,1)S(1)} %collective-permute-done.1.far_own, bf16[16,32,128]{2,1,0:T(8,128)(2,1)S(1)} %collective-permute-done.2.near_other, ...), custom_call_target="tpu_custom_call" | custom-call | flops 528482304 | bytes 4194304 | tf_op jit(solution)/shard_map/pallas_call | solution.py:347
  23.0 3.3 %collective-permute-done.5.far_a = bf16[6,32,128]{2,1,0:T(8,128)(2,1)S(1)} collective-permute-done((bf16[6,32,128]{2,1,0:T(8,128)(2,1)S(1)}, bf16[6,32,128]{2,1,0:T(8,128)(2,1)S(1)}, u32[]{:S(2)}, u32[]{:S(2)}) %collective-permute-start.5) | collective-permute-done | bytes 49184 | tf_op jit(solution)/shard_map/ppermute | solution.py:333
  26.3 3.4 %shard_map.92 = bf16[16,32,128]{2,1,0:T(8,128)(2,1)S(1)} custom-call(s32[3]{0:T(128)S(1)} %pad_add_fusion.flags, bf16[16,32,128]{2,1,0:T(8,128)(2,1)S(1)} %collective-permute-done.4.near_a, bf16[6,32,128]{2,1,0:T(8,128)(2,1)S(1)} %collective-permute-done.5.far_a, bf16[16,32,128]{2,1,0:T(8,128)(2,1)S(1)} %collective-permute-done.6.near_b, ...), custom_call_target="tpu_custom_call" | custom-call | flops 1509949440 | bytes 4194304 | tf_op jit(solution)/shard_map/pallas_call | solution.py:348
  29.7 0.1 collective-permute-start.8
  29.8 1.3 %collective-permute-done.8 = bf16[2,8,32,128]{3,2,1,0:T(8,128)(2,1)S(1)} collective-permute-done((bf16[2,8,32,128]{3,2,1,0:T(8,128)(2,1)S(1)}, bf16[2,8,32,128]{3,2,1,0:T(8,128)(2,1)S(1)}, u32[]{:S(2)}, u32[]{:S(2)}) %collective-permute-start.8) | collective-permute-done | bytes 131104 | tf_op jit(solution)/shard_map/ppermute | solution.py:361
  31.1 0.7 %select_bitcast_fusion = (bf16[2,1,8,32,128]{4,3,2,1,0:T(8,128)(2,1)}, bf16[2,1,8,32,128]{4,3,2,1,0:T(8,128)(2,1)}) fusion(pred[]{:T(512)S(6)} %eq.16, bf16[2,2,8,32,128]{4,3,2,0,1:T(8,128)(2,1)S(1)} %maximum_select_fusion), kind=kLoop, calls=%fused_computation.9 | loop fusion | flops 131072 | bytes 524289
  (22 shorter events, 0.2 us)
Async XLA Ops:
  0.7 9.1 %copy-start.2 = (bf16[2,3,3,128,128]{4,3,2,1,0:T(8,128)(2,1)S(1)}, bf16[2,3,3,128,128]{4,3,2,1,0:T(8,128)(2,1)}, u32[]{:S(2)}) copy-start(bf16[2,3,3,128,128]{4,3,2,1,0:T(8,128)(2,1)} %refs_0_.7) | copy-start | bytes 1769476
  1.6 1.5 %collective-permute-start = (bf16[8,32,128]{2,1,0:T(8,128)(2,1)S(1)}, bf16[8,32,128]{2,1,0:T(8,128)(2,1)S(1)}, u32[]{:S(2)}, u32[]{:S(2)}) collective-permute-start(bf16[8,32,128]{2,1,0:T(8,128)(2,1)S(1)} %get-tuple-element.27), channel_id=1, source_target_pairs={{0,1},{1,0},{2,3},{3,2},{4,5},{5,4},{6,7},{7,6},{8,9},{9,8},{10,11... | collective-permute-start | bytes 196616 | tf_op jit(solution)/shard_map/ppermute | solution.py:301
  3.1 9.1 %collective-permute-start.2 = (bf16[16,32,128]{2,1,0:T(8,128)(2,1)S(1)}, bf16[16,32,128]{2,1,0:T(8,128)(2,1)S(1)}, u32[]{:S(2)}, u32[]{:S(2)}) collective-permute-start(bf16[16,32,128]{2,1,0:T(8,128)(2,1)S(1)} %maximum_select_fusion.1.near_own), channel_id=1, source_target_pairs={{0,4},{4,0},{8,12},{12,8},{1,5},{5,1},{9,13},{13,9},{2,6},{6,2},{1... | collective-permute-start | bytes 393224 | tf_op jit(solution)/shard_map/ppermute | solution.py:304
  6.1 6.1 %collective-permute-start.3 = (bf16[6,32,128]{2,1,0:T(8,128)(2,1)S(1)}, bf16[6,32,128]{2,1,0:T(8,128)(2,1)S(1)}, u32[]{:S(2)}, u32[]{:S(2)}) collective-permute-start(bf16[6,32,128]{2,1,0:T(8,128)(2,1)S(1)} %constant_dynamic-slice_fusion), channel_id=1, source_target_pairs={{0,6},{1,7},{2,4},{3,5},{4,2},{5,3},{6,0},{7,1},{8,14},{9,15},{10,... | collective-permute-start | bytes 147464 | tf_op jit(solution)/shard_map/ppermute | solution.py:306
  7.5 4.7 %collective-permute-start.1 = (bf16[6,32,128]{2,1,0:T(8,128)(2,1)S(1)}, bf16[6,32,128]{2,1,0:T(8,128)(2,1)S(1)}, u32[]{:S(2)}, u32[]{:S(2)}) collective-permute-start(bf16[6,32,128]{2,1,0:T(8,128)(2,1)S(1)} %constant_dynamic-slice_fusion), channel_id=1, source_target_pairs={{0,2},{2,0},{1,3},{3,1},{4,6},{6,4},{5,7},{7,5},{8,10},{10,8},{9,1... | collective-permute-start | bytes 147464 | tf_op jit(solution)/shard_map/ppermute | solution.py:305
  7.7 1.3 %copy-start = (bf16[2,3,3,256,128]{4,3,2,1,0:T(8,128)(2,1)S(1)}, bf16[2,3,3,256,128]{4,3,2,1,0:T(8,128)(2,1)}, u32[]{:S(2)}) copy-start(bf16[2,3,3,256,128]{4,3,2,1,0:T(8,128)(2,1)} %refs_0_.6) | copy-start | bytes 3538948
  9.0 1.1 %copy-start.3 = (bf16[2,3,3,128,128]{4,3,2,1,0:T(8,128)(2,1)S(1)}, bf16[2,3,3,128,128]{4,3,2,1,0:T(8,128)(2,1)}, u32[]{:S(2)}) copy-start(bf16[2,3,3,128,128]{4,3,2,1,0:T(8,128)(2,1)} %refs_1_.3) | copy-start | bytes 1769476
  10.0 2.1 %copy-start.4 = (f32[2,128]{1,0:T(2,128)S(1)}, f32[2,128]{1,0:T(2,128)}, u32[]{:S(2)}) copy-start(f32[2,128]{1,0:T(2,128)} %b_in.3) | copy-start | bytes 3076
  10.0 2.1 %copy-start.5 = (f32[2,128]{1,0:T(2,128)S(1)}, f32[2,128]{1,0:T(2,128)}, u32[]{:S(2)}) copy-start(f32[2,128]{1,0:T(2,128)} %b_mid.3) | copy-start | bytes 3076
  10.1 2.1 %copy-start.6 = (f32[2,128]{1,0:T(2,128)S(1)}, f32[2,128]{1,0:T(2,128)}, u32[]{:S(2)}) copy-start(f32[2,128]{1,0:T(2,128)} %b_out.3) | copy-start | bytes 3076
  10.8 9.4 %copy-start.1 = (bf16[2,3,3,256,128]{4,3,2,1,0:T(8,128)(2,1)S(1)}, bf16[2,3,3,256,128]{4,3,2,1,0:T(8,128)(2,1)}, u32[]{:S(2)}) copy-start(bf16[2,3,3,256,128]{4,3,2,1,0:T(8,128)(2,1)} %refs_0_.6) | copy-start | bytes 3538948
  15.6 10.7 %collective-permute-start.6 = (bf16[16,32,128]{2,1,0:T(8,128)(2,1)S(1)}, bf16[16,32,128]{2,1,0:T(8,128)(2,1)S(1)}, u32[]{:S(2)}, u32[]{:S(2)}) collective-permute-start(bf16[16,32,128]{2,1,0:T(8,128)(2,1)S(1)} %get-tuple-element.14), channel_id=1, source_target_pairs={{0,1},{1,0},{2,3},{3,2},{4,8},{5,9},{6,10},{7,11},{8,4},{9,5},{10,... | collective-permute-start | bytes 393224 | tf_op jit(solution)/shard_map/ppermute | solution.py:333
  15.7 10.6 %collective-permute-start.4 = (bf16[16,32,128]{2,1,0:T(8,128)(2,1)S(1)}, bf16[16,32,128]{2,1,0:T(8,128)(2,1)S(1)}, u32[]{:S(2)}, u32[]{:S(2)}) collective-permute-start(bf16[16,32,128]{2,1,0:T(8,128)(2,1)S(1)} %get-tuple-element.14), channel_id=1, source_target_pairs={{0,4},{1,5},{2,6},{3,7},{4,12},{5,13},{6,14},{7,15},{8,0},{9,1},{1... | collective-permute-start | bytes 393224 | tf_op jit(solution)/shard_map/ppermute | solution.py:333
  18.8 4.2 %collective-permute-start.7 = (bf16[6,32,128]{2,1,0:T(8,128)(2,1)S(1)}, bf16[6,32,128]{2,1,0:T(8,128)(2,1)S(1)}, u32[]{:S(2)}, u32[]{:S(2)}) collective-permute-start(bf16[6,32,128]{2,1,0:T(8,128)(2,1)S(1)} %get-tuple-element.15), channel_id=1, source_target_pairs={{0,1},{1,0},{2,3},{3,2},{4,10},{5,11},{6,8},{7,9},{8,6},{9,7},{10,... | collective-permute-start | bytes 147464 | tf_op jit(solution)/shard_map/ppermute | solution.py:333
  18.8 7.5 %collective-permute-start.5 = (bf16[6,32,128]{2,1,0:T(8,128)(2,1)S(1)}, bf16[6,32,128]{2,1,0:T(8,128)(2,1)S(1)}, u32[]{:S(2)}, u32[]{:S(2)}) collective-permute-start(bf16[6,32,128]{2,1,0:T(8,128)(2,1)S(1)} %get-tuple-element.15), channel_id=1, source_target_pairs={{0,6},{1,7},{2,4},{3,5},{4,14},{5,15},{6,12},{7,13},{8,2},{9,3},{1... | collective-permute-start | bytes 147464 | tf_op jit(solution)/shard_map/ppermute | solution.py:333
  29.7 1.4 %collective-permute-start.8 = (bf16[2,8,32,128]{3,2,1,0:T(8,128)(2,1)S(1)}, bf16[2,8,32,128]{3,2,1,0:T(8,128)(2,1)S(1)}, u32[]{:S(2)}, u32[]{:S(2)}) collective-permute-start(bf16[2,8,32,128]{3,2,1,0:T(8,128)(2,1)S(1)} %get-tuple-element.25), channel_id=1, source_target_pairs={{0,1},{1,0},{2,3},{3,2},{4,5},{5,4},{6,7},{7,6},{8,9},{9,8},{10,11... | collective-permute-start | bytes 393224 | tf_op jit(solution)/shard_map/ppermute | solution.py:361
